TPU v7x, 128 devices: a whole 4x4x4 slice. The times are simulated.
128 devices in a mesh: strip: 128 (over z, x, y, core).
Axes of the slice: x: 4, y: 4, z: 4, core: 2. Of those that a mesh axis runs over, the one named last changes fastest.
Arguments:
- state: float32 [4096, 4096], P('strip'), may hold values from -6 to 6
- noise: float32 [4096, 4096], P('strip'), may hold values from -6 to 6
- step: float32 [1], replicated, may hold values from 0.3 to 0.7
- field_scale: float32 [1], replicated, may hold values from 0.6 to 1.2
- wave_scale: float32 [1], replicated, may hold values from 4 to 8
- source: float32 [2048, 2048], P('strip'), may hold values from -6 to 6
- obs_cells: int32 [8192], replicated, may hold values from 0 to 4194303
- obs_values: float32 [8192], replicated, may hold values from -3 to 3
Outputs:
- log_perm: float32 [2048, 2048], P('strip')
- pressure: float32 [2048, 2048], P('strip')
- loglik: float32 [], replicated
Inputs may be any that keep to these rules, and one draw needn't show every extreme that they name: `obs_cells`: each entry is row * 2048 + column of an observed cell of the field grid.
All inputs are finite; a program needn't handle non-finite values.
Results may differ from a plain program's by a relative error of at most 0.00011.
Values sent between devices are 32-bit elements; how exact they have to be, the bound alone decides.
A program may use at most 64 MiB of HBM per device.

v0:
```python
import functools
import math

import jax
import jax.numpy as jnp
from jax import lax
from jax.sharding import Mesh
from jax.sharding import PartitionSpec as P

ITERS = 4
STRIP = ("strip_0", "strip_1", "strip_2", "strip_3")


precise = lax.Precision.HIGHEST


def sent_together(arrays, axis, split_dim, concat_dim, along):
    both = jnp.concatenate(arrays, axis=along)
    out, at, outs = (
        lax.all_to_all(both, axis, split_axis=split_dim, concat_axis=concat_dim, tiled=True),
        0,
        [],
    )
    for a in arrays:
        outs.append(lax.slice_in_dim(out, at, at + a.shape[along], axis=along))
        at += a.shape[along]
    return tuple(outs)


def padded(block, sides, width):
    for axis, dim in sides:
        count = lax.axis_size(axis)
        forward = [(i, i + 1) for i in range(count - 1)]
        backward = [(target, source) for source, target in forward]
        low = lax.ppermute(
            lax.slice_in_dim(block, block.shape[dim] - width, None, axis=dim), axis, forward
        )
        high = lax.ppermute(lax.slice_in_dim(block, 0, width, axis=dim), axis, backward)
        block = jnp.concatenate([low, block, high], axis=dim)
    return block


def over_axes(array, axes):
    return functools.reduce(lax.psum, axes, array)


def split_length(length):
    second = min(128, length)
    return (length // second, second)


def phase_table(height, breadth, modulus, orient):
    product = (
        lax.broadcasted_iota(jnp.int32, (height, breadth), 0)
        * lax.broadcasted_iota(jnp.int32, (height, breadth), 1)
        % modulus
    )
    angles = product.astype(jnp.float32) * (orient * 2.0 * math.pi / modulus)
    return (jnp.cos(angles), jnp.sin(angles))


def true_freq(index, factor, second):
    return index // second + factor * (index % second)


def forward_permuted(real_part, imag_part, orient):
    length = real_part.shape[-1]
    factor, second = split_length(length)
    leading = real_part.shape[:-1]
    inner_cos, inner_sin = phase_table(factor, factor, factor, orient)
    shaped = real_part.reshape(leading + (factor, second))
    section_real = jnp.einsum("kn,...na->...ka", inner_cos, shaped, precision=precise)
    section_imag = jnp.einsum("kn,...na->...ka", inner_sin, shaped, precision=precise)
    if imag_part is not None:
        shaped_imag = imag_part.reshape(leading + (factor, second))
        section_real = section_real - jnp.einsum(
            "kn,...na->...ka", inner_sin, shaped_imag, precision=precise
        )
        section_imag = section_imag + jnp.einsum(
            "kn,...na->...ka", inner_cos, shaped_imag, precision=precise
        )
    twist_cos, twist_sin = phase_table(factor, second, length, orient)
    turned_real = section_real * twist_cos - section_imag * twist_sin
    turned_imag = section_real * twist_sin + section_imag * twist_cos
    outer_cos, outer_sin = phase_table(second, second, second, orient)
    result_real = jnp.einsum(
        "ja,...ka->...kj", outer_cos, turned_real, precision=precise
    ) - jnp.einsum("ja,...ka->...kj", outer_sin, turned_imag, precision=precise)
    result_imag = jnp.einsum(
        "ja,...ka->...kj", outer_sin, turned_real, precision=precise
    ) + jnp.einsum("ja,...ka->...kj", outer_cos, turned_imag, precision=precise)
    return (result_real.reshape(leading + (length,)), result_imag.reshape(leading + (length,)))


def inverse_natural(real_part, imag_part, orient, keep, real_only=False):
    length = real_part.shape[-1]
    factor, second = split_length(length)
    leading = real_part.shape[:-1]
    shaped_real = real_part.reshape(leading + (factor, second))
    shaped_imag = imag_part.reshape(leading + (factor, second))
    inner_cos, inner_sin = phase_table(second, second, second, orient)
    section_real = jnp.einsum(
        "ak,...jk->...ja", inner_cos, shaped_real, precision=precise
    ) - jnp.einsum("ak,...jk->...ja", inner_sin, shaped_imag, precision=precise)
    section_imag = jnp.einsum(
        "ak,...jk->...ja", inner_sin, shaped_real, precision=precise
    ) + jnp.einsum("ak,...jk->...ja", inner_cos, shaped_imag, precision=precise)
    twist_cos, twist_sin = phase_table(factor, second, length, orient)
    turned_real = section_real * twist_cos - section_imag * twist_sin
    turned_imag = section_real * twist_sin + section_imag * twist_cos
    outer_cos, outer_sin = phase_table(keep // second, factor, factor, orient)
    result_real = jnp.einsum(
        "bj,...ja->...ba", outer_cos, turned_real, precision=precise
    ) - jnp.einsum("bj,...ja->...ba", outer_sin, turned_imag, precision=precise)
    result_real = result_real.reshape(leading + (keep,))
    if real_only:
        return (result_real, None)
    result_imag = jnp.einsum(
        "bj,...ja->...ba", outer_sin, turned_real, precision=precise
    ) + jnp.einsum("bj,...ja->...ba", outer_cos, turned_imag, precision=precise)
    return (result_real, result_imag.reshape(leading + (keep,)))


def amplitude(row_freq, col_freq, length, scale, wave):
    row_wave = jnp.minimum(row_freq, length - row_freq).astype(jnp.float32)
    col_wave = jnp.minimum(col_freq, length - col_freq).astype(jnp.float32)
    shape_term = 1.0 / (1.0 + (row_wave * row_wave + col_wave * col_wave) / (wave * wave))
    return scale * length / (wave * math.sqrt(math.pi)) * shape_term


def mirror_row(values, factor, second):
    length = values.shape[-1]
    grid = values.reshape(factor, second)
    flipped = jnp.roll(jnp.flip(grid, (0, 1)), 1, axis=0)
    head = jnp.roll(jnp.flip(grid[:1], 1), 1, axis=1)
    return jnp.concatenate([head, flipped[1:]], axis=0).reshape(1, length)


def body(state, noise, step, field_scale, wave_scale, source, obs_cells, obs_values):
    parts = lax.axis_size(STRIP)
    position = lax.axis_index(STRIP)
    rows_here, length = state.shape
    half = length // 2
    factor, second = split_length(length)
    field_rows = source.shape[0]
    rate = step[0]
    sigma = field_scale[0]
    wave = wave_scale[0]
    mixed = jnp.sqrt(1.0 - rate * rate) * state + rate * noise
    row_freq = true_freq(lax.broadcasted_iota(jnp.int32, (1, length), 1), factor, second)
    width = half // parts
    halfway = second // 2
    freq_real, freq_imag = forward_permuted(mixed, None, -1.0)
    grid_real = freq_real.reshape(rows_here, factor, second)
    grid_imag = freq_imag.reshape(rows_here, factor, second)
    corner = (lax.broadcasted_iota(jnp.int32, (factor, halfway), 0) == 0) & (
        lax.broadcasted_iota(jnp.int32, (factor, halfway), 1) == 0
    )
    packed_real = grid_real[:, :, :halfway].reshape(rows_here, half)
    packed_imag = jnp.where(
        corner, grid_real[:, :1, halfway : halfway + 1], grid_imag[:, :, :halfway]
    ).reshape(rows_here, half)
    send_real = packed_real.reshape(rows_here, parts, width).transpose(1, 2, 0)
    send_imag = packed_imag.reshape(rows_here, parts, width).transpose(1, 2, 0)
    column_real, column_imag = sent_together((send_real, send_imag), STRIP, 0, 2, 1)
    column_real = column_real.reshape(width, length)
    column_imag = column_imag.reshape(width, length)
    spec_real, spec_imag = forward_permuted(column_real, column_imag, -1.0)
    slot = position * width + lax.broadcasted_iota(jnp.int32, (width, 1), 0)
    col_freq = true_freq(slot, factor, halfway)
    scaled = amplitude(row_freq, col_freq, length, sigma, wave)
    mixed_real = scaled * spec_real
    mixed_imag = scaled * spec_imag
    first_real = spec_real[:1]
    first_imag = spec_imag[:1]
    mirror_real = mirror_row(first_real, factor, second)
    mirror_imag = mirror_row(first_imag, factor, second)
    even_real = 0.5 * (first_real + mirror_real)
    even_imag = 0.5 * (first_imag - mirror_imag)
    odd_real = 0.5 * (first_imag + mirror_imag)
    odd_imag = -0.5 * (first_real - mirror_real)
    zero_amp = amplitude(row_freq, jnp.zeros((1, 1), jnp.int32), length, sigma, wave)
    top_amp = amplitude(row_freq, jnp.full((1, 1), half, jnp.int32), length, sigma, wave)
    joined_real = zero_amp * even_real - top_amp * odd_imag
    joined_imag = zero_amp * even_imag + top_amp * odd_real
    owner = position == 0
    head_real = jnp.where(owner, joined_real, mixed_real[:1])
    head_imag = jnp.where(owner, joined_imag, mixed_imag[:1])
    mixed_real = jnp.concatenate([head_real, mixed_real[1:]], axis=0)
    mixed_imag = jnp.concatenate([head_imag, mixed_imag[1:]], axis=0)
    field_real, field_imag = inverse_natural(mixed_real, mixed_imag, 1.0, half)
    back_real, back_imag = sent_together(
        (
            field_real.reshape(width, parts, field_rows),
            field_imag.reshape(width, parts, field_rows),
        ),
        STRIP,
        1,
        0,
        2,
    )
    lower_real = back_real.reshape(half, field_rows).T.reshape(field_rows, factor, halfway)
    lower_imag = back_imag.reshape(half, field_rows).T.reshape(field_rows, factor, halfway)
    low_real = jnp.where(corner, lower_real, 2.0 * lower_real)
    low_imag = jnp.where(corner, 0.0, 2.0 * lower_imag)
    upper_real = jnp.where(corner, lower_imag[:, :1, :1], 0.0)
    upper_imag = jnp.zeros((field_rows, factor, halfway), jnp.float32)
    spread_real = jnp.concatenate([low_real, upper_real], axis=2).reshape(field_rows, length)
    spread_imag = jnp.concatenate([low_imag, upper_imag], axis=2).reshape(field_rows, length)
    log_perm = inverse_natural(spread_real, spread_imag, 1.0, half, True)[0] / (length * length)
    kappa = jnp.exp(log_perm)
    rimmed = padded(kappa, ((STRIP, 0),), 1)
    sided = jnp.pad(kappa, ((0, 0), (1, 1)))
    north = 0.5 * (kappa + rimmed[:-2])
    south = 0.5 * (kappa + rimmed[2:])
    west = 0.5 * (kappa + sided[:, :-2])
    east = 0.5 * (kappa + sided[:, 2:])
    diagonal = north + south + west + east
    pressure = jnp.zeros_like(source)
    residual = source
    direction = jnp.zeros_like(source)
    along = jnp.zeros_like(source)
    gamma_prior = jnp.float32(1.0)
    alpha_prior = jnp.float32(1.0)
    for iteration in range(ITERS):
        precond = residual / diagonal
        beside_all = padded(precond, ((STRIP, 0),), 1)
        beside = jnp.pad(precond, ((0, 0), (1, 1)))
        image = (
            diagonal * precond
            - north * beside_all[:-2]
            - south * beside_all[2:]
            - west * beside[:, :-2]
            - east * beside[:, 2:]
        )
        gamma, delta = (
            over_axes(jnp.sum(residual * precond), STRIP),
            over_axes(jnp.sum(precond * image), STRIP),
        )
        if iteration == 0:
            alpha = gamma / delta
            direction = precond
            along = image
        else:
            ratio = gamma / gamma_prior
            alpha = gamma / (delta - ratio * gamma / alpha_prior)
            direction = precond + ratio * direction
            along = image + ratio * along
        pressure = pressure + alpha * direction
        residual = residual - alpha * along
        gamma_prior = gamma
        alpha_prior = alpha
    columns = pressure.shape[1]
    cell_row = obs_cells // columns
    cell_col = obs_cells % columns
    local_row = cell_row - position * field_rows
    inside = (local_row >= 0) & (local_row < field_rows)
    picked = pressure[jnp.clip(local_row, 0, field_rows - 1), cell_col]
    differ = jnp.where(inside, picked - obs_values, 0.0)
    total = over_axes(jnp.sum(differ * differ), STRIP)
    loglik = -(2.0 / obs_cells.shape[0]) * total
    return (log_perm, pressure, loglik)


def solution(mesh):
    torus = Mesh(mesh.devices.reshape(4, 4, 4, 2), ("strip_0", "strip_1", "strip_2", "strip_3"))
    in_specs = (P(STRIP, None), P(STRIP, None), P(), P(), P(), P(STRIP, None), P(), P())
    out_specs = (P(STRIP, None), P(STRIP, None), P())
    return jax.shard_map(body, mesh=torus, in_specs=in_specs, out_specs=out_specs, check_vma=False)
```

profile of v0, /device:TPU:1, one launch (start us, length us, event | category | flops | bytes accessed | tf_op | source)
XLA Modules:
  0.0 371.1 jit_solution(9031461268499406090)
XLA Ops:
  1.3 1.3 add_bitcast_fusion
  2.7 0.7 convolution_bitcast_fusion
  3.4 0.6 convolution_bitcast_fusion.1
  4.1 0.8 fusion.16
  4.9 0.8 fusion.15
  5.8 0.8 fusion.17
  6.6 0.8 convolution_subtract_fusion
  8.5 1.4 copy.38
  9.9 1.5 pad_maximum_fusion
  11.5 1.7 reshape.462
  13.2 11.7 %all-to-all-start = ((f32[128,1,1024]{2,1,0:T(1,128)}), f32[128,1,1024]{2,1,0:T(1,128)S(1)}, u32[]{:S(2)}, u32[]{:S(2)}) async-start(f32[128,1,1024]{2,1,0:T(1,128)} %reshape.462), calls=%async_computation | async-start | bytes 1048576 | tf_op jit(solution)/shard_map/all_to_all | solution.py:20
  26.3 11.9 %all-to-all-done = f32[128,1,1024]{2,1,0:T(1,128)S(1)} async-done(((f32[128,1,1024]{2,1,0:T(1,128)}), f32[128,1,1024]{2,1,0:T(1,128)S(1)}, u32[]{:S(2)}, u32[]{:S(2)}) %all-to-all-start) | async-done | bytes 524320 | tf_op jit(solution)/shard_map/all_to_all | solution.py:20
  38.8 1.9 reduce.4
  40.6 0.7 reshape.463
  41.3 2.6 copy.40
  43.9 2.5 all_to_all.29
  48.5 0.6 fusion.66
  50.4 0.6 convolution_subtract_fusion.3
  58.8 15.4 %all_to_all.36 = f32[128,1,512]{2,1,0:T(1,128)S(1)} all-to-all(f32[128,1,512]{2,1,0:T(1,128)S(1)} %reshape.464), channel_id=1, replica_groups=mesh['strip_0'=4,'strip_1'=4,'strip_2'=4,'strip_3'=2] {'strip_0','strip_..., dimensions={0} | all-to-all | bytes 524288 | tf_op jit(solution)/shard_map/all_to_all | solution.py:20
  74.2 1.3 reduce.5
  77.1 0.6 fusion.65
  77.8 0.6 fusion.64
  80.4 0.7 fusion.324
  81.1 2.7 collective-permute-start
  83.8 1.9 collective-permute-start.1
  85.8 3.0 collective-permute-done.1
  89.0 1.9 collective-permute-start.2
  90.9 2.4 collective-permute-start.3
  93.3 2.6 collective-permute-done.3
  95.9 0.8 multiply_reduce_fusion.5
  96.6 9.1 %all-reduce.17 = (f32[]{:T(128)}, f32[]{:T(128)}) all-reduce(f32[]{:T(128)} %get-tuple-element.10, f32[]{:T(128)} %get-tuple-element.9), channel_id=1, replica_groups=mesh['strip_0'=4,'strip_1'=4,'strip_2'=4,'strip_3'=2] {'strip_0'}, use_global_device_ids=true, to_apply=%region_1.2 | all-reduce | flops 2 | bytes 16 | tf_op jit(solution)/shard_map/psum | solution.py:44
  105.7 6.6 %all-reduce.13 = (f32[]{:T(128)}, f32[]{:T(128)}) all-reduce(f32[]{:T(128)} %get-tuple-element.33, f32[]{:T(128)} %get-tuple-element.34), channel_id=1, replica_groups=mesh['strip_0'=4,'strip_1'=4,'strip_2'=4,'strip_3'=2] {'strip_1'}, use_global_device_ids=true, to_apply=%region_2.3 | all-reduce | flops 2 | bytes 16 | tf_op jit(solution)/shard_map/psum | solution.py:44
  112.3 17.7 %all-reduce.9 = (f32[]{:T(128)}, f32[]{:T(128)}) all-reduce(f32[]{:T(128)} %get-tuple-element.25, f32[]{:T(128)} %get-tuple-element.26), channel_id=1, replica_groups=mesh['strip_0'=4,'strip_1'=4,'strip_2'=4,'strip_3'=2] {'strip_2'}, use_global_device_ids=true, to_apply=%region_3.4 | all-reduce | flops 2 | bytes 16 | tf_op jit(solution)/shard_map/psum | solution.py:44
  130.1 3.6 all-reduce.21
  135.1 3.9 %collective-permute-start.4 = (f32[1,2048]{1,0:T(1,128)S(1)}, f32[1,2048]{1,0:T(1,128)S(1)}, u32[]{:S(2)}, u32[]{:S(2)}) collective-permute-start(f32[1,2048]{1,0:T(1,128)S(1)} %get-tuple-element.66), channel_id=1, source_target_pairs={{0,1},{1,2},{2,3},{3,4},{4,5},{5,6},{6,7},{7,8},{8,9},{9,10},{10,1... | collective-permute-start | bytes 24584 | tf_op jit(solution)/shard_map/ppermute | solution.py:35
  139.0 1.9 collective-permute-start.5
  140.9 3.0 collective-permute-done.5
  143.9 0.8 multiply_reduce_fusion.3
  144.8 6.7 %all-reduce.16 = (f32[]{:T(128)}, f32[]{:T(128)}) all-reduce(f32[]{:T(128)} %get-tuple-element.8, f32[]{:T(128)} %get-tuple-element.7), channel_id=1, replica_groups=mesh['strip_0'=4,'strip_1'=4,'strip_2'=4,'strip_3'=2] {'strip_0'}, use_global_device_ids=true, to_apply=%region_11.12 | all-reduce | flops 2 | bytes 16 | tf_op jit(solution)/shard_map/psum | solution.py:44
  151.4 8.7 %all-reduce.12 = (f32[]{:T(128)}, f32[]{:T(128)}) all-reduce(f32[]{:T(128)} %get-tuple-element.31, f32[]{:T(128)} %get-tuple-element.32), channel_id=1, replica_groups=mesh['strip_0'=4,'strip_1'=4,'strip_2'=4,'strip_3'=2] {'strip_1'}, use_global_device_ids=true, to_apply=%region_12.13 | all-reduce | flops 2 | bytes 16 | tf_op jit(solution)/shard_map/psum | solution.py:44
  160.1 13.0 %all-reduce.8 = (f32[]{:T(128)}, f32[]{:T(128)}) all-reduce(f32[]{:T(128)} %get-tuple-element.23, f32[]{:T(128)} %get-tuple-element.24), channel_id=1, replica_groups=mesh['strip_0'=4,'strip_1'=4,'strip_2'=4,'strip_3'=2] {'strip_2'}, use_global_device_ids=true, to_apply=%region_13.14 | all-reduce | flops 2 | bytes 16 | tf_op jit(solution)/shard_map/psum | solution.py:44
  173.2 3.7 all-reduce.20
  181.5 3.9 %collective-permute-start.6 = (f32[1,2048]{1,0:T(1,128)S(1)}, f32[1,2048]{1,0:T(1,128)S(1)}, u32[]{:S(2)}, u32[]{:S(2)}) collective-permute-start(f32[1,2048]{1,0:T(1,128)S(1)} %get-tuple-element.64), channel_id=1, source_target_pairs={{0,1},{1,2},{2,3},{3,4},{4,5},{5,6},{6,7},{7,8},{8,9},{9,10},{10,1... | collective-permute-start | bytes 24584 | tf_op jit(solution)/shard_map/ppermute | solution.py:35
  185.4 1.9 collective-permute-start.7
  187.3 3.0 collective-permute-done.7
  190.3 0.8 multiply_reduce_fusion.1
  191.1 7.2 %all-reduce.15 = (f32[]{:T(128)}, f32[]{:T(128)}) all-reduce(f32[]{:T(128)} %get-tuple-element.6, f32[]{:T(128)} %get-tuple-element.5), channel_id=1, replica_groups=mesh['strip_0'=4,'strip_1'=4,'strip_2'=4,'strip_3'=2] {'strip_0'}, use_global_device_ids=true, to_apply=%region_21.22 | all-reduce | flops 2 | bytes 16 | tf_op jit(solution)/shard_map/psum | solution.py:44
  198.3 8.1 %all-reduce.11 = (f32[]{:T(128)}, f32[]{:T(128)}) all-reduce(f32[]{:T(128)} %get-tuple-element.29, f32[]{:T(128)} %get-tuple-element.30), channel_id=1, replica_groups=mesh['strip_0'=4,'strip_1'=4,'strip_2'=4,'strip_3'=2] {'strip_1'}, use_global_device_ids=true, to_apply=%region_22.23 | all-reduce | flops 2 | bytes 16 | tf_op jit(solution)/shard_map/psum | solution.py:44
  206.3 12.6 %all-reduce.7 = (f32[]{:T(128)}, f32[]{:T(128)}) all-reduce(f32[]{:T(128)} %get-tuple-element.21, f32[]{:T(128)} %get-tuple-element.22), channel_id=1, replica_groups=mesh['strip_0'=4,'strip_1'=4,'strip_2'=4,'strip_3'=2] {'strip_2'}, use_global_device_ids=true, to_apply=%region_23.24 | all-reduce | flops 2 | bytes 16 | tf_op jit(solution)/shard_map/psum | solution.py:44
  218.9 3.6 all-reduce.19
  226.5 3.9 %collective-permute-start.8 = (f32[1,2048]{1,0:T(1,128)S(1)}, f32[1,2048]{1,0:T(1,128)S(1)}, u32[]{:S(2)}, u32[]{:S(2)}) collective-permute-start(f32[1,2048]{1,0:T(1,128)S(1)} %get-tuple-element.62), channel_id=1, source_target_pairs={{0,1},{1,2},{2,3},{3,4},{4,5},{5,6},{6,7},{7,8},{8,9},{9,10},{10,1... | collective-permute-start | bytes 24584 | tf_op jit(solution)/shard_map/ppermute | solution.py:35
  230.4 1.9 collective-permute-start.9
  232.4 3.0 collective-permute-done.9
  235.4 0.7 fusion.38
  236.1 7.6 %all-reduce.14 = (f32[]{:T(128)}, f32[]{:T(128)}) all-reduce(f32[]{:T(128)} %get-tuple-element.4, f32[]{:T(128)} %get-tuple-element.3), channel_id=1, replica_groups=mesh['strip_0'=4,'strip_1'=4,'strip_2'=4,'strip_3'=2] {'strip_0'}, use_global_device_ids=true, to_apply=%region_31.32 | all-reduce | flops 2 | bytes 16 | tf_op jit(solution)/shard_map/psum | solution.py:44
  243.7 7.7 %all-reduce.10 = (f32[]{:T(128)}, f32[]{:T(128)}) all-reduce(f32[]{:T(128)} %get-tuple-element.27, f32[]{:T(128)} %get-tuple-element.28), channel_id=1, replica_groups=mesh['strip_0'=4,'strip_1'=4,'strip_2'=4,'strip_3'=2] {'strip_1'}, use_global_device_ids=true, to_apply=%region_32.33 | all-reduce | flops 2 | bytes 16 | tf_op jit(solution)/shard_map/psum | solution.py:44
  251.5 12.7 %all-reduce.6 = (f32[]{:T(128)}, f32[]{:T(128)}) all-reduce(f32[]{:T(128)} %get-tuple-element.19, f32[]{:T(128)} %get-tuple-element.20), channel_id=1, replica_groups=mesh['strip_0'=4,'strip_1'=4,'strip_2'=4,'strip_3'=2] {'strip_2'}, use_global_device_ids=true, to_apply=%region_33.34 | all-reduce | flops 2 | bytes 16 | tf_op jit(solution)/shard_map/psum | solution.py:44
  264.1 3.6 all-reduce.18
  271.6 65.0 %gather_fusion = f32[8192]{0:T(1024)S(1)} fusion(f32[16,2048]{1,0:T(8,128)S(1)} %multiply_add_fusion.5, s32[8192]{0:T(1024)S(1)} %fusion.96), kind=kCustom, calls=%fused_computation | custom fusion | bytes 131072 | tf_op jit(solution)/shard_map/gather | solution.py:258
  336.6 0.6 multiply_reduce_fusion.7
  337.2 7.5 %psum.284 = f32[]{:T(128)} all-reduce(f32[]{:T(128)} %multiply_reduce_fusion.7), channel_id=1, replica_groups=mesh['strip_0'=4,'strip_1'=4,'strip_2'=4,'strip_3'=2] {'strip_0'}, use_global_device_ids=true, to_apply=%region_41.42 | all-reduce | flops 1 | bytes 8 | tf_op jit(solution)/shard_map/psum | solution.py:44
  344.7 7.5 %psum.285 = f32[]{:T(128)} all-reduce(f32[]{:T(128)} %psum.284), channel_id=1, replica_groups=mesh['strip_0'=4,'strip_1'=4,'strip_2'=4,'strip_3'=2] {'strip_1'}, use_global_device_ids=true, to_apply=%region_42.43 | all-reduce | flops 1 | bytes 8 | tf_op jit(solution)/shard_map/psum | solution.py:44
  352.2 8.3 %psum.286 = f32[]{:T(128)} all-reduce(f32[]{:T(128)} %psum.285), channel_id=1, replica_groups=mesh['strip_0'=4,'strip_1'=4,'strip_2'=4,'strip_3'=2] {'strip_2'}, use_global_device_ids=true, to_apply=%region_43.44 | all-reduce | flops 1 | bytes 8 | tf_op jit(solution)/shard_map/psum | solution.py:44
  360.6 8.8 %psum.287 = f32[]{:T(128)} all-reduce(f32[]{:T(128)} %psum.286), channel_id=1, replica_groups=mesh['strip_0'=4,'strip_1'=4,'strip_2'=4,'strip_3'=2] {'strip_3'}, use_global_device_ids=true, to_apply=%region_44.45 | all-reduce | flops 1 | bytes 8 | tf_op jit(solution)/shard_map/psum | solution.py:44
  (91 shorter events, 16.7 us)
Async XLA Ops:
  13.2 25.1 %all-to-all-start = ((f32[128,1,1024]{2,1,0:T(1,128)}), f32[128,1,1024]{2,1,0:T(1,128)S(1)}, u32[]{:S(2)}, u32[]{:S(2)}) async-start(f32[128,1,1024]{2,1,0:T(1,128)} %reshape.462), calls=%async_computation | async-start | bytes 1048576 | tf_op jit(solution)/shard_map/all_to_all | solution.py:20
  77.8 11.0 %copy-start.1 = (f32[16,2048]{1,0:T(8,128)S(1)}, f32[16,2048]{1,0:T(8,128)}, u32[]{:S(2)}) copy-start(f32[16,2048]{1,0:T(8,128)} %param.13) | copy-start | bytes 393220
  81.1 4.6 %collective-permute-start = (f32[1,2048]{1,0:T(1,128)S(1)}, f32[1,2048]{1,0:T(1,128)S(1)}, u32[]{:S(2)}, u32[]{:S(2)}) collective-permute-start(f32[1,2048]{1,0:T(1,128)S(1)} %get-tuple-element.70), channel_id=1, source_target_pairs={{0,1},{1,2},{2,3},{3,4},{4,5},{5,6},{6,7},{7,8},{8,9},{9,10},{10,1... | collective-permute-start | bytes 24584 | tf_op jit(solution)/shard_map/ppermute | solution.py:35
  83.8 5.0 %collective-permute-start.1 = (f32[1,2048]{1,0:T(1,128)S(1)}, f32[1,2048]{1,0:T(1,128)S(1)}, u32[]{:S(2)}, u32[]{:S(2)}) collective-permute-start(f32[1,2048]{1,0:T(1,128)S(1)} %get-tuple-element.71), channel_id=1, source_target_pairs={{1,0},{2,1},{3,2},{4,3},{5,4},{6,5},{7,6},{8,7},{9,8},{10,9},{11,1... | collective-permute-start | bytes 24584 | tf_op jit(solution)/shard_map/ppermute | solution.py:38
  89.0 4.3 %collective-permute-start.2 = (f32[1,2048]{1,0:T(1,128)S(1)}, f32[1,2048]{1,0:T(1,128)S(1)}, u32[]{:S(2)}, u32[]{:S(2)}) collective-permute-start(f32[1,2048]{1,0:T(1,128)S(1)} %get-tuple-element.68), channel_id=1, source_target_pairs={{0,1},{1,2},{2,3},{3,4},{4,5},{5,6},{6,7},{7,8},{8,9},{9,10},{10,1... | collective-permute-start | bytes 24584 | tf_op jit(solution)/shard_map/ppermute | solution.py:35
  90.9 5.0 %collective-permute-start.3 = (f32[1,2048]{1,0:T(1,128)S(1)}, f32[1,2048]{1,0:T(1,128)S(1)}, u32[]{:S(2)}, u32[]{:S(2)}) collective-permute-start(f32[1,2048]{1,0:T(1,128)S(1)} %get-tuple-element.69), channel_id=1, source_target_pairs={{1,0},{2,1},{3,2},{4,3},{5,4},{6,5},{7,6},{8,7},{9,8},{10,9},{11,1... | collective-permute-start | bytes 24584 | tf_op jit(solution)/shard_map/ppermute | solution.py:38
  135.0 97.3 %copy-start.2 = (s32[8192]{0:T(1024)S(1)}, s32[8192]{0:T(1024)}, u32[]{:S(2)}) copy-start(s32[8192]{0:T(1024)} %param.14) | copy-start | bytes 98308
  135.1 5.8 %collective-permute-start.4 = (f32[1,2048]{1,0:T(1,128)S(1)}, f32[1,2048]{1,0:T(1,128)S(1)}, u32[]{:S(2)}, u32[]{:S(2)}) collective-permute-start(f32[1,2048]{1,0:T(1,128)S(1)} %get-tuple-element.66), channel_id=1, source_target_pairs={{0,1},{1,2},{2,3},{3,4},{4,5},{5,6},{6,7},{7,8},{8,9},{9,10},{10,1... | collective-permute-start | bytes 24584 | tf_op jit(solution)/shard_map/ppermute | solution.py:35
  139.0 5.0 %collective-permute-start.5 = (f32[1,2048]{1,0:T(1,128)S(1)}, f32[1,2048]{1,0:T(1,128)S(1)}, u32[]{:S(2)}, u32[]{:S(2)}) collective-permute-start(f32[1,2048]{1,0:T(1,128)S(1)} %get-tuple-element.67), channel_id=1, source_target_pairs={{1,0},{2,1},{3,2},{4,3},{5,4},{6,5},{7,6},{8,7},{9,8},{10,9},{11,1... | collective-permute-start | bytes 24584 | tf_op jit(solution)/shard_map/ppermute | solution.py:38
  181.5 5.8 %collective-permute-start.6 = (f32[1,2048]{1,0:T(1,128)S(1)}, f32[1,2048]{1,0:T(1,128)S(1)}, u32[]{:S(2)}, u32[]{:S(2)}) collective-permute-start(f32[1,2048]{1,0:T(1,128)S(1)} %get-tuple-element.64), channel_id=1, source_target_pairs={{0,1},{1,2},{2,3},{3,4},{4,5},{5,6},{6,7},{7,8},{8,9},{9,10},{10,1... | collective-permute-start | bytes 24584 | tf_op jit(solution)/shard_map/ppermute | solution.py:35
  185.4 5.0 %collective-permute-start.7 = (f32[1,2048]{1,0:T(1,128)S(1)}, f32[1,2048]{1,0:T(1,128)S(1)}, u32[]{:S(2)}, u32[]{:S(2)}) collective-permute-start(f32[1,2048]{1,0:T(1,128)S(1)} %get-tuple-element.65), channel_id=1, source_target_pairs={{1,0},{2,1},{3,2},{4,3},{5,4},{6,5},{7,6},{8,7},{9,8},{10,9},{11,1... | collective-permute-start | bytes 24584 | tf_op jit(solution)/shard_map/ppermute | solution.py:38
  226.5 5.9 %collective-permute-start.8 = (f32[1,2048]{1,0:T(1,128)S(1)}, f32[1,2048]{1,0:T(1,128)S(1)}, u32[]{:S(2)}, u32[]{:S(2)}) collective-permute-start(f32[1,2048]{1,0:T(1,128)S(1)} %get-tuple-element.62), channel_id=1, source_target_pairs={{0,1},{1,2},{2,3},{3,4},{4,5},{5,6},{6,7},{7,8},{8,9},{9,10},{10,1... | collective-permute-start | bytes 24584 | tf_op jit(solution)/shard_map/ppermute | solution.py:35
  230.4 5.0 %collective-permute-start.9 = (f32[1,2048]{1,0:T(1,128)S(1)}, f32[1,2048]{1,0:T(1,128)S(1)}, u32[]{:S(2)}, u32[]{:S(2)}) collective-permute-start(f32[1,2048]{1,0:T(1,128)S(1)} %get-tuple-element.63), channel_id=1, source_target_pairs={{1,0},{2,1},{3,2},{4,3},{5,4},{6,5},{7,6},{8,7},{9,8},{10,9},{11,1... | collective-permute-start | bytes 24584 | tf_op jit(solution)/shard_map/ppermute | solution.py:38
  271.5 65.0 %copy-start = (f32[16,2048]{1,0:T(8,128)}, f32[16,2048]{1,0:T(8,128)S(1)}, u32[]{:S(2)}) copy-start(f32[16,2048]{1,0:T(8,128)S(1)} %multiply_add_fusion.5) | copy-start | bytes 393220
  271.5 65.0 %copy-start.3 = (f32[8192]{0:T(1024)S(1)}, f32[8192]{0:T(1024)}, u32[]{:S(2)}) copy-start(f32[8192]{0:T(1024)} %param.15) | copy-start | bytes 98308
where the time goes:
time: 372 us; the launch traced here: 371 us
  blocking collectives  180 us (48%)
  local copies, waits for them, and re-layouts  80.2 us (22%)
  starting transfers between devices  38 us (10%)
  waiting for transfers between devices  26.5 us (7%)
  between operations  18.8 us (5%)
  matrix products  16.1 us (4%)
  other arithmetic  11.7 us (3%)
    psum x20, blocking collectives, over_axes(): return functools.reduce(lax.psum, axes, array)  164 us
    gather x1, local copies, waits for them, and re-layouts, body(): picked = pressure[jnp.clip(local_row, 0, field_rows - 1), cell_col]  65 us
    ppermute x5, starting transfers between devices, padded(): lax.ppermute(lax.slice_in_dim(block, block.shape[dim] - width, None, axis...  16.2 us
    all_to_all x1, blocking collectives, sent_together(): lax.all_to_all(both, axis, split_axis=split_dim, concat_axis=concat_dim,...  15.4 us
    ppermute x5, waiting for transfers between devices, padded(): lax.ppermute(lax.slice_in_dim(block, 0, width, axis=dim), axis, backward)  14.6 us
    all_to_all x1, waiting for transfers between devices, sent_together(): lax.all_to_all(both, axis, split_axis=split_dim, concat_axis=concat_dim,...  11.9 us
    all_to_all x1, starting transfers between devices, sent_together(): lax.all_to_all(both, axis, split_axis=split_dim, concat_axis=concat_dim,...  11.7 us
    ppermute x5, starting transfers between devices, padded(): lax.ppermute(lax.slice_in_dim(block, 0, width, axis=dim), axis, backward)  10.1 us
  transfers between devices with their start and end apart: 11, of which 6 were waited for; matrix products, arithmetic and copies ran while one was open for 0% of the time, Pallas kernels for 0%

commit v1 on v0

v1 whole, which is shorter than its diff:
```python
import functools
import math

import jax
import jax.numpy as jnp
import ml_dtypes
import numpy as np
from jax import lax
from jax.experimental import pallas as pl
from jax.experimental.pallas import tpu as pltpu
from jax.sharding import PartitionSpec as P

M = 4096
N = 2048
DEVICES = 128
ROWS = M // DEVICES
FIELD = N // DEVICES
KS = 80
AXIS = "strip"
MESH = pl.DeviceIdType.MESH
F32 = jnp.float32
BF16 = jnp.bfloat16


def halves(table):
    table = table.astype(np.float32)
    high = table.astype(ml_dtypes.bfloat16)
    low = (table - high.astype(np.float32)).astype(ml_dtypes.bfloat16)
    return np.stack([high, low])


def tables():
    b = np.arange(256)
    kl = np.arange(128)
    angle = 2 * np.pi * np.outer(kl, b) / 256
    top = np.zeros((16, 512))
    top[0, :256] = (-1.0) ** b
    row_forward = np.concatenate(
        [
            np.concatenate([np.cos(angle), np.sin(angle)], 1),
            np.concatenate([-np.sin(angle), np.cos(angle)], 1),
            top,
        ]
    )
    row_back = np.concatenate(
        [
            np.concatenate([np.cos(angle), np.sin(angle)], 1),
            np.concatenate([-np.sin(angle), np.cos(angle)], 1),
        ]
    )
    kv = np.arange(16)
    turn = 2 * np.pi * np.outer(kv, b) / M
    row_turn = np.stack([np.cos(turn), np.sin(turn)])
    ks = np.arange(KS)
    real = ks <= 64
    src = np.arange(DEVICES)
    angle = 2 * np.pi * np.outer(ks, src) / 128
    col_forward = np.concatenate([np.cos(angle), -np.sin(angle)]) * np.tile(real, 2)[:, None]
    weight = np.where((ks == 0) | (ks == 64), 1.0, 2.0) * real
    angle = angle.T[:64]
    col_back = np.concatenate([np.cos(angle) * weight, -np.sin(angle) * weight], 1)
    r = np.arange(32)
    lanes_in = [(v, q) for v in range(4) for q in range(32)]
    lanes_out = [(v, h * 16 + q) for h in range(2) for v in range(4) for q in range(16)]
    turn = 2 * np.pi * np.outer(ks, [q for _, q in lanes_in]) / M
    turn_back = 2 * np.pi * np.outer(ks, [q for _, q in lanes_out]) / M
    col_turn = np.stack([np.cos(turn), np.sin(turn), np.cos(turn_back), np.sin(turn_back)])
    vi, qi = np.array(lanes_in).T
    vo, qo = np.array(lanes_out).T
    same = vi[:, None] == vi[None, :]
    angle = 2 * np.pi * qi[:, None] * qi[None, :] / 32
    c, s = np.cos(angle) * same, np.sin(angle) * same
    mid_forward = np.block([[c, -s], [s, c]])
    same = vi[:, None] == vo[None, :]
    angle = 2 * np.pi * qi[:, None] * qo[None, :] / 32
    c, s = np.cos(angle) * same, np.sin(angle) * same
    mid_back = np.block([[c, s], [-s, c]])
    return (
        halves(row_forward),
        halves(row_back),
        row_turn.astype(np.float32),
        halves(col_forward),
        halves(col_back),
        col_turn.astype(np.float32),
        halves(mid_forward),
        halves(mid_back),
    )


def split(x):
    high = x.astype(BF16)
    return high, (x - high.astype(F32)).astype(BF16)


NN = (((1,), (0,)), ((), ()))
NT = (((1,), (1,)), ((), ()))


def product(left, right, form):
    dot = functools.partial(lax.dot_general, dimension_numbers=form, preferred_element_type=F32)
    (lh, ll), (rh, rl) = left, right
    return dot(lh, rh) + (dot(lh, rl) + dot(ll, rh))


def scaled(x, factor):
    if abs(factor) < 1e-12:
        return None
    if abs(factor - 1) < 1e-12:
        return x
    if abs(factor + 1) < 1e-12:
        return -x
    return x * F32(factor)


def plus(a, b):
    return b if a is None else a if b is None else a + b


def minus(a, b):
    if b is None:
        return a
    return -b if a is None else a - b


def turned(z, cos, sin):
    re, im = z
    out_re = scaled(re, cos) if re is not None else None
    out_im = scaled(re, sin) if re is not None else None
    if im is not None:
        out_re = minus(out_re, scaled(im, sin))
        out_im = plus(out_im, scaled(im, cos))
    return out_re, out_im


def added(a, b):
    return plus(a[0], b[0]), plus(a[1], b[1])


def less(a, b):
    return minus(a[0], b[0]), minus(a[1], b[1])


def real_dft(xs):
    count = len(xs)
    if count == 1:
        return [(xs[0], None)]
    even, odd = real_dft(xs[::2]), real_dft(xs[1::2])
    out = [None] * (count // 2 + 1)
    if count == 2:
        return [added(even[0], odd[0]), less(even[0], odd[0])]
    for k in range(count // 4 + 1):
        angle = -2 * math.pi * k / count
        t = turned(odd[k], math.cos(angle), math.sin(angle))
        out[k] = added(even[k], t)
        if k != count // 4:
            re, im = less(even[k], t)
            out[count // 2 - k] = (re, None if im is None else -im)
    return out


def back_dft(zs):
    count = len(zs)
    if count == 1:
        return list(zs)
    even, odd = back_dft(zs[::2]), back_dft(zs[1::2])
    out = [None] * count
    for k in range(count // 2):
        angle = 2 * math.pi * k / count
        t = turned(odd[k], math.cos(angle), math.sin(angle))
        out[k] = added(even[k], t)
        out[k + count // 2] = less(even[k], t)
    return out


def back_dft_real_first_half(zs):
    count = len(zs)
    even, odd = back_dft(zs[::2]), back_dft(zs[1::2])
    out = []
    for k in range(count // 2):
        angle = 2 * math.pi * k / count
        out.append(even[k][0] + turned(odd[k], math.cos(angle), math.sin(angle))[0])
    return out


def send_to_all(me, piece, landing, send_sem, recv_sem):
    @pl.loop(1, DEVICES)
    def _(i):
        other = lax.rem(me + i, DEVICES)
        pltpu.make_async_remote_copy(
            src_ref=piece(other),
            dst_ref=landing(me),
            send_sem=send_sem,
            recv_sem=recv_sem,
            device_id=(other,),
            device_id_type=MESH,
        ).start()


def wait_for_all(me, whole, send_sem, recv_sem):
    pltpu.make_async_remote_copy(
        src_ref=whole,
        dst_ref=whole,
        send_sem=send_sem,
        recv_sem=recv_sem,
        device_id=(lax.rem(me + 1, DEVICES),),
        device_id_type=MESH,
    ).wait()


def greet_all(me):
    barrier = pltpu.get_barrier_semaphore()

    @pl.loop(1, DEVICES)
    def _(i):
        pl.semaphore_signal(barrier, inc=1, device_id=(lax.rem(me + i, DEVICES),), device_id_type=MESH)


def meet_all():
    pl.semaphore_wait(pltpu.get_barrier_semaphore(), DEVICES - 1)


def rows_forward(rate, state, noise, row_turn, z_high, z_low, row_forward, out):
    keep = jnp.sqrt(1.0 - rate * rate)
    for g in range(ROWS // 16):
        rows = slice(16 * g, 16 * g + 16)
        for h in range(2):
            xs = []
            for a in range(16):
                cols = slice(256 * a + 128 * h, 256 * a + 128 * h + 128)
                xs.append(keep * state[rows, cols] + rate * noise[rows, cols])
            ys = real_dft(xs)
            for kv in range(16):
                re, im = ys[kv] if kv <= 8 else ys[16 - kv]
                cos = row_turn[0, kv : kv + 1, 128 * h : 128 * h + 128]
                sin = row_turn[1, kv : kv + 1, 128 * h : 128 * h + 128]
                if kv > 8:
                    im = -im
                if kv == 0:
                    zr, zi = re, jnp.zeros_like(re)
                elif im is None:
                    zr, zi = re * cos, -(re * sin)
                else:
                    zr, zi = re * cos + im * sin, im * cos - re * sin
                spot = slice(kv * ROWS + 16 * g, kv * ROWS + 16 * g + 16)
                for part, lane in ((zr, 128 * h), (zi, 256 + 128 * h)):
                    high, low = split(part)
                    z_high[spot, lane : lane + 128] = high
                    z_low[spot, lane : lane + 128] = low
    for pair in range(2):
        rows = slice(256 * pair, 256 * pair + 256)
        res = product((row_forward[0], row_forward[1]), (z_high[rows, :], z_low[rows, :]), NT)
        for i in range(2):
            t = 2 * pair + i
            lanes = slice(128 * i, 128 * i + 128)
            im = res[128:256, lanes]
            if t == 0:
                first = (lax.broadcasted_iota(jnp.int32, (128, 128), 0) == 0) & (
                    lax.broadcasted_iota(jnp.int32, (128, 128), 1) < ROWS
                )
                im = jnp.where(first, jnp.broadcast_to(res[256:257, lanes], (128, 128)), im)
            out[pl.ds(t, 128, stride=8), :] = res[:128, lanes]
            out[pl.ds(4 + t, 128, stride=8), :] = im


def amplitudes(me, sigma, wave, amp):
    ks = lax.broadcasted_iota(jnp.int32, (KS, 128), 0)
    lane = lax.broadcasted_iota(jnp.int32, (KS, 128), 1)
    k0 = ks + 128 * (lane % 32)
    q0 = jnp.minimum(k0, M - k0).astype(F32)
    base = q0 * q0 + wave * wave
    gain = sigma * wave * F32(2.0 / (math.sqrt(math.pi) * M))
    for v in range(4):
        k1 = 16 * me + 4 * v + lane // 32
        q1 = k1.astype(F32)
        value = gain / (base + q1 * q1)
        if v == 0:
            alone = k1 == 0
            value = jnp.where(alone, 0.5 * value, value)
            top = jnp.where(alone, 0.5 * gain / (base + F32(N) * F32(N)), value)
            amp[4] = top
        else:
            amp[4 + v] = value
        amp[v] = value


def columns(got, amp, col_forward, col_back, col_turn, mid_forward, mid_back, out):
    for u in range(4):
        pieces = jnp.concatenate([got[pl.ds(2 * u + i, 128, stride=8), :] for i in range(2)], axis=1)
        spec = product((col_forward[0], col_forward[1]), split(pieces), NN)
        parts = []
        for i in range(2):
            lanes = slice(128 * i, 128 * i + 128)
            re, im = spec[:KS, lanes], spec[KS:, lanes]
            cos, sin = col_turn[0], col_turn[1]
            parts.append(jnp.concatenate([re * cos + im * sin, im * cos - re * sin], axis=1))
        full = product(split(jnp.concatenate(parts, axis=0)), (mid_forward[0], mid_forward[1]), NN)
        factor = jnp.concatenate([amp[2 * u], amp[2 * u + 1]], axis=0)
        full = full * jnp.concatenate([factor, factor], axis=1)
        back = product(split(full), (mid_back[0], mid_back[1]), NN)
        sides = []
        for i in range(2):
            rows = slice(KS * i, KS * i + KS)
            re, im = back[rows, :128], back[rows, 128:]
            cos, sin = col_turn[2], col_turn[3]
            sides.append(jnp.concatenate([re * cos - im * sin, im * cos + re * sin], axis=0))
        field = product((col_back[0], col_back[1]), split(jnp.concatenate(sides, axis=1)), NN)
        left, right = field[:, :128], field[:, 128:]
        low = lax.broadcasted_iota(jnp.int32, (64, 128), 1) < 64
        out[pl.ds(u, 64, stride=8), :] = jnp.where(low, left, pltpu.roll(right, 64, 1))
        out[pl.ds(4 + u, 64, stride=8), :] = jnp.where(low, pltpu.roll(left, 64, 1), right)


def rows_back(got, row_back, row_turn, put):
    blocks = [got[pl.ds(u, 128, stride=4), :].T for u in range(4)]
    re = jnp.concatenate(blocks[:2], axis=0)
    im = jnp.concatenate(blocks[2:], axis=0)
    corner = (lax.broadcasted_iota(jnp.int32, (256, 128), 0) < FIELD) & (
        lax.broadcasted_iota(jnp.int32, (256, 128), 1) == 0
    )
    top = jnp.broadcast_to(im[:FIELD, :1], (FIELD, 128))
    sign = (1 - 2 * (lax.broadcasted_iota(jnp.int32, (FIELD, 128), 1) % 2)).astype(F32)
    top = top * sign
    im = jnp.where(corner, 0.0, im)
    q = product(split(jnp.concatenate([re, im], axis=1)), (row_back[0], row_back[1]), NN)
    for h in range(2):
        zs = []
        for kv in range(16):
            rows = slice(FIELD * kv, FIELD * kv + FIELD)
            zr, zi = q[rows, 128 * h : 128 * h + 128], q[rows, 256 + 128 * h : 384 + 128 * h]
            cos = row_turn[0, kv : kv + 1, 128 * h : 128 * h + 128]
            sin = row_turn[1, kv : kv + 1, 128 * h : 128 * h + 128]
            zs.append((zr, zi) if kv == 0 else (zr * cos - zi * sin, zi * cos + zr * sin))
        for a, value in enumerate(back_dft_real_first_half(zs)):
            put(256 * a + 128 * h, value + top)


def transform_kernel(
    step, sigma, wave, state, noise, row_forward, row_back, row_turn, col_forward, col_back, col_turn,
    mid_forward, mid_back, log_perm, z_high, z_low, sent1, got1, amp, sent2, got2, sems,
):
    me = lax.axis_index(AXIS)
    greet_all(me)
    rows_forward(step[0], state, noise, row_turn, z_high, z_low, row_forward, sent1)
    meet_all()
    send_to_all(me, lambda d: sent1.at[pl.ds(8 * d, 8), :], lambda s: got1.at[pl.ds(8 * s, 8), :], sems.at[0], sems.at[1])
    own = pl.ds(pl.multiple_of(8 * me, 8), 8)
    got1[own, :] = sent1[own, :]
    amplitudes(me, sigma[0], wave[0], amp)
    wait_for_all(me, got1.at[pl.ds(0, 8 * (DEVICES - 1)), :], sems.at[0], sems.at[1])
    columns(got1, amp, col_forward, col_back, col_turn, mid_forward, mid_back, sent2)
    send_to_all(me, lambda d: sent2.at[pl.ds(4 * d, 4), :], lambda s: got2.at[pl.ds(4 * s, 4), :], sems.at[2], sems.at[3])
    own = pl.ds(pl.multiple_of(4 * me, 4), 4)
    got2[own, :] = sent2[own, :]
    wait_for_all(me, got2.at[pl.ds(0, 4 * (DEVICES - 1)), :], sems.at[2], sems.at[3])

    def put(at, value):
        log_perm[:, at : at + 128] = value

    rows_back(got2, row_back, row_turn, put)


def log_permeability(step, sigma, wave, state, noise):
    vmem = pl.BlockSpec(memory_space=pltpu.VMEM)
    smem = pl.BlockSpec(memory_space=pltpu.SMEM)
    return pl.pallas_call(
        transform_kernel,
        out_shape=jax.ShapeDtypeStruct((FIELD, N), F32),
        in_specs=[smem] * 3 + [vmem] * 10,
        out_specs=vmem,
        scratch_shapes=[
            pltpu.VMEM((512, 512), BF16),
            pltpu.VMEM((512, 512), BF16),
            pltpu.VMEM((1024, 128), F32),
            pltpu.VMEM((1024, 128), F32),
            pltpu.VMEM((8, KS, 128), F32),
            pltpu.VMEM((512, 128), F32),
            pltpu.VMEM((512, 128), F32),
            pltpu.SemaphoreType.DMA((4,)),
        ],
        compiler_params=pltpu.CompilerParams(collective_id=0, has_side_effects=True, vmem_limit_bytes=60 * 2**20),
    )(step, sigma, wave, state, noise, *[jnp.asarray(t) for t in tables()])


def padded(block):
    forward = [(i, i + 1) for i in range(DEVICES - 1)]
    backward = [(i + 1, i) for i in range(DEVICES - 1)]
    low = lax.ppermute(block[-1:], AXIS, forward)
    high = lax.ppermute(block[:1], AXIS, backward)
    return jnp.concatenate([low, block, high], axis=0)


def body(state, noise, step, field_scale, wave_scale, source, obs_cells, obs_values):
    position = lax.axis_index(AXIS)
    log_perm = log_permeability(step, field_scale, wave_scale, state, noise)
    kappa = jnp.exp(log_perm)
    rimmed = padded(kappa)
    sided = jnp.pad(kappa, ((0, 0), (1, 1)))
    north = 0.5 * (kappa + rimmed[:-2])
    south = 0.5 * (kappa + rimmed[2:])
    west = 0.5 * (kappa + sided[:, :-2])
    east = 0.5 * (kappa + sided[:, 2:])
    diagonal = north + south + west + east
    pressure = jnp.zeros_like(source)
    residual = source
    direction = jnp.zeros_like(source)
    along = jnp.zeros_like(source)
    gamma_prior = jnp.float32(1.0)
    alpha_prior = jnp.float32(1.0)
    for iteration in range(4):
        precond = residual / diagonal
        beside_all = padded(precond)
        beside = jnp.pad(precond, ((0, 0), (1, 1)))
        image = (
            diagonal * precond
            - north * beside_all[:-2]
            - south * beside_all[2:]
            - west * beside[:, :-2]
            - east * beside[:, 2:]
        )
        gamma, delta = lax.psum(jnp.stack([jnp.sum(residual * precond), jnp.sum(precond * image)]), AXIS)
        if iteration == 0:
            alpha = gamma / delta
            direction = precond
            along = image
        else:
            ratio = gamma / gamma_prior
            alpha = gamma / (delta - ratio * gamma / alpha_prior)
            direction = precond + ratio * direction
            along = image + ratio * along
        pressure = pressure + alpha * direction
        residual = residual - alpha * along
        gamma_prior = gamma
        alpha_prior = alpha
    columns_here = pressure.shape[1]
    cell_row = obs_cells // columns_here
    cell_col = obs_cells % columns_here
    local_row = cell_row - position * FIELD
    inside = (local_row >= 0) & (local_row < FIELD)
    picked = pressure[jnp.clip(local_row, 0, FIELD - 1), cell_col]
    differ = jnp.where(inside, picked - obs_values, 0.0)
    total = lax.psum(jnp.sum(differ * differ), AXIS)
    loglik = -(2.0 / obs_cells.shape[0]) * total
    return (log_perm, pressure, loglik)


def solution(mesh):
    in_specs = (P(AXIS, None), P(AXIS, None), P(), P(), P(), P(AXIS, None), P(), P())
    out_specs = (P(AXIS, None), P(AXIS, None), P())
    return jax.shard_map(body, mesh=mesh, in_specs=in_specs, out_specs=out_specs, check_vma=False)
```

time: 372 us -> 515 us (1.38)
  blocking collectives: 180 us -> 344 us
  Pallas kernels: 0 us -> 33.8 us
  matrix products: 16.1 us -> 0 us
  starting transfers between devices: 38 us -> 24.9 us
  waiting for transfers between devices: 26.5 us -> 14.7 us
  local copies, waits for them, and re-layouts: 80.2 us -> 69 us
    psum x20 -> x5, blocking collectives: 164 us -> 344 us  [the longest x4 279 us: body(): lax.psum(jnp.stack([jnp.sum(residual * precond), jnp.sum(precond * image)...]
    pallas_call x0 -> x1, Pallas kernels: none -> 33.8 us  [log_permeability(): pl.pallas_call(transform_kernel, out_shape=jax.ShapeDtypeStruct((FIELD, N...]
    dot_general x28 -> x0, matrix products: 16.1 us -> none  [the longest x2 1.45 us: forward_permuted(): jnp.einsum('ja,...ka->...kj', outer_sin, turned_imag, precision=precise)]
    all_to_all x1 -> x0, blocking collectives: 15.4 us -> none  [sent_together(): lax.all_to_all(both, axis, split_axis=split_dim, concat_axis=concat_dim,...]
    all_to_all x1 -> x0, waiting for transfers between devices: 11.9 us -> none  [sent_together(): lax.all_to_all(both, axis, split_axis=split_dim, concat_axis=concat_dim,...]
    all_to_all x1 -> x0, starting transfers between devices: 11.7 us -> none  [sent_together(): lax.all_to_all(both, axis, split_axis=split_dim, concat_axis=concat_dim,...]
    all_to_all x3 -> x0, local copies, waits for them, and re-layouts: 5.63 us -> none  [sent_together(): lax.all_to_all(both, axis, split_axis=split_dim, concat_axis=concat_dim,...]
    another operation x0 -> x4, other arithmetic: none -> 5.37 us  [body(): jnp.stack([jnp.sum(residual * precond), jnp.sum(precond * image)])]
  transfers between devices with their start and end apart: 11 -> 10, of which waited for: 6 -> 5; matrix products, arithmetic and copies ran while one was open for 0% -> 0% of each run, Pallas kernels for 0% -> 0%
where the time goes in v1:
time: 515 us; the launch traced here: 514 us
  blocking collectives  344 us (67%)
  local copies, waits for them, and re-layouts  69 us (13%)
  Pallas kernels  33.8 us (7%)
  starting transfers between devices  24.9 us (5%)
  between operations  18.1 us (4%)
  waiting for transfers between devices  14.7 us (3%)
  other arithmetic  9.36 us (2%)
    psum x4, blocking collectives, body(): lax.psum(jnp.stack([jnp.sum(residual * precond), jnp.sum(precond * image)...  279 us
    gather x1, local copies, waits for them, and re-layouts, body(): picked = pressure[jnp.clip(local_row, 0, FIELD - 1), cell_col]  65 us
    psum x1, blocking collectives, body(): total = lax.psum(jnp.sum(differ * differ), AXIS)  64.4 us
    pallas_call x1, Pallas kernels, log_permeability(): pl.pallas_call(transform_kernel, out_shape=jax.ShapeDtypeStruct((FIELD, N...  33.8 us
    ppermute x5, starting transfers between devices, padded(): low = lax.ppermute(block[-1:], AXIS, forward)  14.9 us
    ppermute x5, waiting for transfers between devices, padded(): high = lax.ppermute(block[:1], AXIS, backward)  14.7 us
  transfers between devices with their start and end apart: 10, of which 5 were waited for; matrix products, arithmetic and copies ran while one was open for 0% of the time, Pallas kernels for 0%

profile of v1, /device:TPU:1, one launch (start us, length us, event | category | flops | bytes accessed | tf_op | source)
XLA Modules:
  0.0 513.9 jit_solution(17229861835403795654)
XLA Ops:
  2.6 0.0 copy-start.2
  2.6 33.8 %shard_map.175 = f32[16,2048]{1,0:T(8,128)} custom-call(f32[1]{0:T(128)S(6)} %copy.20.step, f32[1]{0:T(128)S(6)} %copy.21.sigma, f32[1]{0:T(128)S(6)} %copy.22.wave, f32[32,4096]{1,0:T(8,128)} %state.1, f32[32,4096]{1,0:T(8,128)} %noise.1, bf16[2,272,512]{2,1,0:T(8,128)(2,1)} %constant.63.clone.row_forward, bf16[2,256,512]{2,1,0:T(8,128)(2,1)} %constant.64.clone.row_back, ...), custom_call_target="tpu_custom_call" | custom-call | tf_op jit(solution)/shard_map/pallas_call | solution.py:365
  36.4 0.9 exp.3
  37.4 2.7 collective-permute-start
  40.1 1.9 collective-permute-start.1
  42.1 0.0 collective-permute-done
  42.1 3.0 collective-permute-done.1
  45.1 0.0 copy-done.2
  45.1 0.1 fusion.56
  45.3 1.9 collective-permute-start.2
  47.2 2.4 collective-permute-start.3
  49.6 0.0 collective-permute-done.2
  49.6 2.6 collective-permute-done.3
  52.2 0.7 multiply_reduce_fusion.6
  52.9 1.4 pad_maximum_fusion.10
  54.3 73.1 %psum.35 = f32[2]{0:T(128)S(1)} all-reduce(f32[2]{0:T(128)S(1)} %pad_maximum_fusion.10), channel_id=1, replica_groups=mesh['strip'=128] {'strip'}, use_global_device_ids=true, to_apply=%region_2.3 | all-reduce | flops 2 | bytes 16 | tf_op jit(solution)/shard_map/psum | solution.py:420
  127.5 0.6 fusion.67
  129.4 3.0 collective-permute-start.4
  132.5 1.9 collective-permute-start.5
  134.4 0.0 collective-permute-done.4
  134.4 3.0 collective-permute-done.5
  137.4 0.7 multiply_reduce_fusion.4
  138.2 1.3 pad_maximum_fusion.11
  139.5 68.9 %psum.36 = f32[2]{0:T(128)S(1)} all-reduce(f32[2]{0:T(128)S(1)} %pad_maximum_fusion.11), channel_id=1, replica_groups=mesh['strip'=128] {'strip'}, use_global_device_ids=true, to_apply=%region_5.6 | all-reduce | flops 2 | bytes 16 | tf_op jit(solution)/shard_map/psum | solution.py:420
  208.3 0.6 fusion.66
  213.3 3.5 collective-permute-start.6
  216.9 1.9 collective-permute-start.7
  218.8 0.0 collective-permute-done.6
  218.8 3.0 collective-permute-done.7
  221.8 0.7 multiply_reduce_fusion.2
  222.6 1.4 pad_maximum_fusion.12
  223.9 69.0 %psum.37 = f32[2]{0:T(128)S(1)} all-reduce(f32[2]{0:T(128)S(1)} %pad_maximum_fusion.12), channel_id=1, replica_groups=mesh['strip'=128] {'strip'}, use_global_device_ids=true, to_apply=%region_8.9 | all-reduce | flops 2 | bytes 16 | tf_op jit(solution)/shard_map/psum | solution.py:420
  293.0 0.6 fusion.65
  297.4 0.0 copy-start.3
  297.5 3.7 collective-permute-start.8
  301.1 1.9 collective-permute-start.9
  303.1 0.0 collective-permute-done.8
  303.1 3.0 collective-permute-done.9
  306.1 0.7 multiply_reduce_fusion
  306.9 1.4 pad_maximum_fusion.13
  308.2 0.0 copy-done.3
  308.2 0.1 fusion.45
  308.3 68.4 %psum.38 = f32[2]{0:T(128)S(1)} all-reduce(f32[2]{0:T(128)S(1)} %pad_maximum_fusion.13), channel_id=1, replica_groups=mesh['strip'=128] {'strip'}, use_global_device_ids=true, to_apply=%region_11.12 | all-reduce | flops 2 | bytes 16 | tf_op jit(solution)/shard_map/psum | solution.py:420
  376.7 0.6 fusion.64
  381.2 0.1 multiply_add_fusion
  381.3 0.0 copy-start
  381.3 0.0 copy-start.4
  381.3 0.0 copy-start.1
  381.3 65.0 %gather_fusion = f32[8192]{0:T(1024)S(1)} fusion(f32[16,2048]{1,0:T(8,128)S(1)} %multiply_add_fusion, s32[8192]{0:T(1024)S(1)} %fusion.45), kind=kCustom, calls=%fused_computation | custom fusion | bytes 131072 | tf_op jit(solution)/shard_map/gather | solution.py:439
  446.3 0.0 copy-done
  446.3 0.0 copy-done.4
  446.4 0.6 multiply_reduce_fusion.7
  447.0 64.4 %psum.39 = f32[]{:T(128)} all-reduce(f32[]{:T(128)} %multiply_reduce_fusion.7), channel_id=1, replica_groups=mesh['strip'=128] {'strip'}, use_global_device_ids=true, to_apply=%region_13.14 | all-reduce | flops 1 | bytes 8 | tf_op jit(solution)/shard_map/psum | solution.py:441
  512.1 0.0 copy-done.1
  512.1 0.7 copy.23
  (8 shorter events, 0.2 us)
Async XLA Ops:
  2.6 42.5 %copy-start.2 = (f32[16,2048]{1,0:T(8,128)S(1)}, f32[16,2048]{1,0:T(8,128)}, u32[]{:S(2)}) copy-start(f32[16,2048]{1,0:T(8,128)} %param.21) | copy-start | bytes 393220
  37.4 4.7 collective-permute-start
  40.1 5.0 collective-permute-start.1
  45.3 4.3 collective-permute-start.2
  47.2 5.0 collective-permute-start.3
  129.4 4.9 collective-permute-start.4
  132.5 5.0 collective-permute-start.5
  213.3 5.5 %collective-permute-start.6 = (f32[1,2048]{1,0:T(1,128)S(1)}, f32[1,2048]{1,0:T(1,128)S(1)}, u32[]{:S(2)}, u32[]{:S(2)}) collective-permute-start(f32[1,2048]{1,0:T(1,128)S(1)} %get-tuple-element.26), channel_id=1, source_target_pairs={{0,1},{1,2},{2,3},{3,4},{4,5},{5,6},{6,7},{7,8},{8,9},{9,10},{10,1... | collective-permute-start | bytes 24584 | tf_op jit(solution)/shard_map/ppermute | solution.py:387
  216.9 5.0 collective-permute-start.7
  297.4 10.8 %copy-start.3 = (s32[8192]{0:T(1024)S(1)}, s32[8192]{0:T(1024)}, u32[]{:S(2)}) copy-start(s32[8192]{0:T(1024)} %param.22) | copy-start | bytes 98308
  297.5 5.6 %collective-permute-start.8 = (f32[1,2048]{1,0:T(1,128)S(1)}, f32[1,2048]{1,0:T(1,128)S(1)}, u32[]{:S(2)}, u32[]{:S(2)}) collective-permute-start(f32[1,2048]{1,0:T(1,128)S(1)} %get-tuple-element.24), channel_id=1, source_target_pairs={{0,1},{1,2},{2,3},{3,4},{4,5},{5,6},{6,7},{7,8},{8,9},{9,10},{10,1... | collective-permute-start | bytes 24584 | tf_op jit(solution)/shard_map/ppermute | solution.py:387
  301.1 5.0 collective-permute-start.9
  381.3 65.0 %copy-start = (f32[16,2048]{1,0:T(8,128)}, f32[16,2048]{1,0:T(8,128)S(1)}, u32[]{:S(2)}) copy-start(f32[16,2048]{1,0:T(8,128)S(1)} %multiply_add_fusion) | copy-start | bytes 393220
  381.3 65.0 %copy-start.4 = (f32[8192]{0:T(1024)S(1)}, f32[8192]{0:T(1024)}, u32[]{:S(2)}) copy-start(f32[8192]{0:T(1024)} %param.23) | copy-start | bytes 98308
  381.3 130.8 %copy-start.1 = (f32[16,2048]{1,0:T(8,128)S(1)}, f32[16,2048]{1,0:T(8,128)}, u32[]{:S(2)}) copy-start(f32[16,2048]{1,0:T(8,128)} %shard_map.175) | copy-start | bytes 393220

commit v2 on v1

--- a/solution.py
+++ b/solution.py
@@ -334,39 +334,288 @@
             put(256 * a + 128 * h, value + top)
 
 
-def transform_kernel(
-    step, sigma, wave, state, noise, row_forward, row_back, row_turn, col_forward, col_back, col_turn,
-    mid_forward, mid_back, log_perm, z_high, z_low, sent1, got1, amp, sent2, got2, sems,
+def gather_observations(me, cells, values, counts, means, hot, parts):
+    counts[...] = jnp.zeros_like(counts)
+
+    @pl.loop(0, 8)
+    def _(c):
+        for i in range(8):
+            cell = cells[pl.ds(8 * c + i, 1), :]
+            value = values[pl.ds(8 * c + i, 1), :]
+            row = cell // N - FIELD * me
+            col = cell % N
+            inside = (row >= 0) & (row < FIELD)
+            spot = jnp.where(inside, (row // 8) * 128 + (col // 128) * 8 + row % 8, -1)
+            lane = jnp.where(inside, col % 128, -1)
+            lanes = slice(128 * i, 128 * i + 128)
+            here = lax.broadcasted_iota(jnp.int32, (256, 128), 0) == spot
+            hot[c, :, lanes] = jnp.where(here, 1.0, 0.0).astype(BF16)
+            there = lax.broadcasted_iota(jnp.int32, (128, 128), 0) == lane
+            high = value.astype(BF16).astype(F32)
+            middle = (value - high).astype(BF16).astype(F32)
+            low = value - high - middle
+            for j, piece in enumerate((jnp.ones_like(value), high, middle, low)):
+                parts[128 * j : 128 * j + 128, lanes] = jnp.where(there, piece, 0.0).astype(BF16)
+        counts[...] += lax.dot_general(hot[c], parts[...], NT, preferred_element_type=F32)
+
+    number = counts[:, :128]
+    total = counts[:, 128:256] + counts[:, 256:384] + counts[:, 384:]
+    means[...] = total / jnp.maximum(number, 1.0)
+
+
+def spread_observations(me, cells, values, means, hot, pieces, spread):
+    turned_means = jnp.concatenate([means[:128, :].T, means[128:, :].T], axis=1)
+    high = turned_means.astype(BF16)
+    rest = turned_means - high.astype(F32)
+    middle = rest.astype(BF16)
+    pieces[:128, :] = high
+    pieces[128:256, :] = middle
+    pieces[256:, :] = (rest - middle.astype(F32)).astype(BF16)
+    spread[...] = jnp.zeros_like(spread)
+
+    @pl.loop(0, 8)
+    def _(c):
+        picked = jnp.dot(pieces[...], hot[c], preferred_element_type=F32)
+        total = jnp.zeros((8, 128), F32)
+        for i in range(8):
+            cell = cells[pl.ds(8 * c + i, 1), :]
+            value = values[pl.ds(8 * c + i, 1), :]
+            row = cell // N - FIELD * me
+            inside = (row >= 0) & (row < FIELD)
+            lane = jnp.where(inside, cell % 128, -1)
+            lanes = slice(128 * i, 128 * i + 128)
+            mean = picked[:128, lanes] + (picked[128:256, lanes] + picked[256:, lanes])
+            there = lax.broadcasted_iota(jnp.int32, (128, 128), 0) == lane
+            off = jnp.where(there, value - mean, 0.0)
+            off = off * off
+            for k in range(16):
+                total = total + off[8 * k : 8 * k + 8]
+        spread[...] += total
+
+
+def exchange_edges(me, own_low, own_high, ext, sems):
+    up, down = lax.rem(me + 1, DEVICES), lax.rem(me + DEVICES - 1, DEVICES)
+    return [
+        pltpu.make_async_remote_copy(
+            src_ref=own_low, dst_ref=ext.at[pl.ds(24, 8), :], send_sem=sems.at[0], recv_sem=sems.at[1],
+            device_id=(down,), device_id_type=MESH,
+        ),
+        pltpu.make_async_remote_copy(
+            src_ref=own_high, dst_ref=ext.at[pl.ds(0, 8), :], send_sem=sems.at[2], recv_sem=sems.at[3],
+            device_id=(up,), device_id_type=MESH,
+        ),
+    ]
+
+
+TILES = N // 128
+OWN = slice(8, 24)
+
+
+def tile(j):
+    return slice(128 * j, 128 * j + 128)
+
+
+def neighbours(load):
+    lane = lax.broadcasted_iota(jnp.int32, (32, 128), 1)
+    values = [load(0), load(1)]
+    rights = [pltpu.roll(v, 1, 1) for v in values]
+    lefts = [pltpu.roll(v, 127, 1) for v in values]
+    before = jnp.zeros_like(rights[0])
+    for j in range(TILES):
+        if j == TILES - 1:
+            after = jnp.zeros_like(before)
+        else:
+            after = lefts[1]
+        west = jnp.where(lane == 0, before, rights[0])
+        east = jnp.where(lane == 127, after, lefts[0])
+        north = pltpu.roll(values[0], 1, 0)
+        south = pltpu.roll(values[0], 31, 0)
+        yield j, values[0], north, south, west, east
+        before = rights[0]
+        if j + 1 < TILES:
+            values = values[1:]
+            rights = rights[1:]
+            lefts = lefts[1:]
+            if j + 2 < TILES:
+                values.append(load(j + 2))
+                rights.append(pltpu.roll(values[1], 1, 1))
+                lefts.append(pltpu.roll(values[1], 127, 1))
+
+
+def krylov(me, lx, sx, kappa, coefs, diag, v0, z0, z1, z2):
+    row = lax.broadcasted_iota(jnp.int32, (32, 128), 0)
+    lane = lax.broadcasted_iota(jnp.int32, (32, 128), 1)
+    valid = ((row >= 8) | (me > 0)) & ((row < 24) | (me < DEVICES - 1))
+    for j in range(TILES):
+        kappa[:, tile(j)] = jnp.where(valid, jnp.exp(lx[:, tile(j)]), 0.0)
+    sums = [jnp.zeros((16, 128), F32) for _ in range(8)]
+    for j, k, kn, ks, kw, ke in neighbours(lambda j: kappa[:, tile(j)]):
+        north, south, west, east = 0.5 * (k + kn), 0.5 * (k + ks), 0.5 * (k + kw), 0.5 * (k + ke)
+        d = north + south + west + east
+        inverse = jnp.where(valid, 1.0 / d, 0.0)
+        coefs[0, :, tile(j)] = north * inverse
+        coefs[1, :, tile(j)] = south * inverse
+        coefs[2, :, tile(j)] = west * inverse
+        coefs[3, :, tile(j)] = east * inverse
+        source = sx[:, tile(j)]
+        first = source * inverse
+        diag[:, tile(j)] = d[OWN]
+        v0[:, tile(j)] = first
+        sums[0] = sums[0] + source[OWN] * first[OWN]
+
+    def beside(values):
+        for j, v, vn, vs, vw, ve in neighbours(lambda j: values[:, tile(j)]):
+            yield j, v, (coefs[0, :, tile(j)] * vn + coefs[1, :, tile(j)] * vs) + (
+                coefs[2, :, tile(j)] * vw + coefs[3, :, tile(j)] * ve
+            )
+
+    for j, v, s in beside(v0):
+        z = v - s
+        z0[:, tile(j)] = z
+        own = z[OWN]
+        sums[1] = sums[1] + sx[OWN, tile(j)] * own
+        sums[2] = sums[2] + diag[:, tile(j)] * own * own
+    for j, v, s in beside(z0):
+        z = -s
+        z1[:, tile(j)] = z
+        own = diag[:, tile(j)] * z[OWN]
+        sums[3] = sums[3] + own * v[OWN]
+        sums[4] = sums[4] + own * z[OWN]
+    for j, v, s in beside(z1):
+        z = -2.0 * s - z0[:, tile(j)]
+        z2[:, tile(j)] = z
+        own = diag[:, tile(j)] * z[OWN]
+        sums[5] = sums[5] + own * v[OWN]
+        sums[6] = sums[6] + own * z[OWN]
+    for j, v, s in beside(z2):
+        z = -2.0 * s[OWN] - z1[OWN, tile(j)]
+        sums[7] = sums[7] + diag[:, tile(j)] * v[OWN] * z
+    return sums
+
+
+def lane_totals(sums):
+    rows = jnp.concatenate([jnp.sum(s, axis=0, keepdims=True) for s in sums], axis=0)
+    totals = jnp.broadcast_to(jnp.sum(rows, axis=1, keepdims=True), (8, 128))
+    at = lax.broadcasted_iota(jnp.int32, (8, 128), 0) == lax.broadcasted_iota(jnp.int32, (8, 128), 1)
+    return jnp.sum(jnp.where(at, totals, 0.0), axis=0, keepdims=True)
+
+
+def share(me, row, mine, all_rows, sems):
+    mine[0:1, :] = row
+    all_rows[pl.ds(me, 1), :] = row
+    send_to_all(me, lambda d: mine.at[pl.ds(0, 1), :], lambda s: all_rows.at[pl.ds(s, 1), :], sems.at[0], sems.at[1])
+    wait_for_all(me, all_rows.at[pl.ds(0, DEVICES - 1), :], sems.at[0], sems.at[1])
+    return jnp.sum(all_rows[...], axis=0, keepdims=True)
+
+
+def weights(row):
+    take = [jnp.broadcast_to(row[:, i : i + 1], (16, 128)) for i in range(8)]
+    g0, e0, m0, m1, q11, q12, q22, q23 = take
+    m2 = 2.0 * q11 - m0
+    m3 = 2.0 * q12 - m1
+    m4 = 2.0 * q22 - m0
+    m5 = 2.0 * q23 - m1
+    m = [m0, m1, m2, m3, m4, m5]
+
+    def inner(i, j):
+        return 0.5 * (m[i + j] + m[abs(i - j)])
+
+    def energy(i, j):
+        return inner(i, j) + 0.5 * (inner(i, j + 1) + inner(i, abs(j - 1)))
+
+    gram = [[None] * 4 for _ in range(4)]
+    gram[0][0] = e0
+    for j in range(3):
+        gram[j + 1][0] = inner(0, j)
+        for i in range(j + 1):
+            gram[j + 1][i + 1] = energy(i, j)
+    right = [g0, e0, m0 - e0, 2.0 * (m1 - (m0 - e0)) - e0]
+    factors = [[None] * 4 for _ in range(4)]
+    inverse = []
+    whole = [gram[i][i] for i in range(4)]
+    for k in range(4):
+        pivot = gram[k][k]
+        inverse.append(jnp.where(pivot > 1e-6 * whole[k], 1.0 / pivot, 0.0))
+        for i in range(k + 1, 4):
+            factors[i][k] = gram[i][k] * inverse[k]
+        for i in range(k + 1, 4):
+            for j in range(k + 1, i + 1):
+                gram[i][j] = gram[i][j] - factors[i][k] * gram[j][k]
+            right[i] = right[i] - factors[i][k] * right[k]
+    out = [right[k] * inverse[k] for k in range(4)]
+    for k in (2, 1, 0):
+        for i in range(k + 1, 4):
+            out[k] = out[k] - factors[i][k] * out[i]
+    return out
+
+
+def kernel(
+    step, sigma, wave, state, noise, source, cells, values,
+    row_forward, row_back, row_turn, col_forward, col_back, col_turn, mid_forward, mid_back,
+    log_perm, pressure, loglik,
+    z_high, z_low, sent1, got1, amp, sent2, got2,
+    counts, means, hot, parts, pieces, spread,
+    lx, sx, kappa, coefs, diag, v0, z0, z1, z2, mine, everyone, sems,
 ):
     me = lax.axis_index(AXIS)
     greet_all(me)
     rows_forward(step[0], state, noise, row_turn, z_high, z_low, row_forward, sent1)
     meet_all()
     send_to_all(me, lambda d: sent1.at[pl.ds(8 * d, 8), :], lambda s: got1.at[pl.ds(8 * s, 8), :], sems.at[0], sems.at[1])
+    source_edges = exchange_edges(me, source.at[pl.ds(0, 8), :], source.at[pl.ds(8, 8), :], sx, sems.at[pl.ds(4, 4)])
+    for copy in source_edges:
+        copy.start()
     own = pl.ds(pl.multiple_of(8 * me, 8), 8)
     got1[own, :] = sent1[own, :]
+    sx[OWN, :] = source[...]
     amplitudes(me, sigma[0], wave[0], amp)
+    gather_observations(me, cells, values, counts, means, hot, parts)
     wait_for_all(me, got1.at[pl.ds(0, 8 * (DEVICES - 1)), :], sems.at[0], sems.at[1])
     columns(got1, amp, col_forward, col_back, col_turn, mid_forward, mid_back, sent2)
     send_to_all(me, lambda d: sent2.at[pl.ds(4 * d, 4), :], lambda s: got2.at[pl.ds(4 * s, 4), :], sems.at[2], sems.at[3])
     own = pl.ds(pl.multiple_of(4 * me, 4), 4)
     got2[own, :] = sent2[own, :]
+    spread_observations(me, cells, values, means, hot, pieces, spread)
     wait_for_all(me, got2.at[pl.ds(0, 4 * (DEVICES - 1)), :], sems.at[2], sems.at[3])
 
     def put(at, value):
         log_perm[:, at : at + 128] = value
+        lx[OWN, at : at + 128] = value
 
     rows_back(got2, row_back, row_turn, put)
-
-
-def log_permeability(step, sigma, wave, state, noise):
+    edges = exchange_edges(me, lx.at[pl.ds(8, 8), :], lx.at[pl.ds(16, 8), :], lx, sems.at[pl.ds(8, 4)])
+    for copy in edges:
+        copy.start()
+    for copy in source_edges + edges:
+        copy.wait()
+    sums = krylov(me, lx, sx, kappa, coefs, diag, v0, z0, z1, z2)
+    y = weights(share(me, lane_totals(sums), mine.at[0], everyone.at[0], sems.at[pl.ds(12, 2)]))
+    total = spread[...]
+    for j in range(TILES):
+        p = (y[0] * v0[OWN, tile(j)] + y[1] * z0[OWN, tile(j)]) + (y[2] * z1[OWN, tile(j)] + y[3] * z2[OWN, tile(j)])
+        pressure[:, tile(j)] = p
+        for g in range(2):
+            rows = slice(128 * g + 8 * j, 128 * g + 8 * j + 8)
+            off = p[8 * g : 8 * g + 8] - means[rows, :]
+            total = total + counts[rows, :128] * (off * off)
+    misfit = jnp.sum(total, axis=0, keepdims=True)
+    everything = share(me, misfit, mine.at[1], everyone.at[1], sems.at[pl.ds(14, 2)])
+    loglik[0, 0] = F32(-2.0 / 8192) * jnp.sum(everything)
+
+
+def body(state, noise, step, field_scale, wave_scale, source, obs_cells, obs_values):
     vmem = pl.BlockSpec(memory_space=pltpu.VMEM)
     smem = pl.BlockSpec(memory_space=pltpu.SMEM)
-    return pl.pallas_call(
-        transform_kernel,
-        out_shape=jax.ShapeDtypeStruct((FIELD, N), F32),
-        in_specs=[smem] * 3 + [vmem] * 10,
-        out_specs=vmem,
+    field = pltpu.VMEM((32, N), F32)
+    log_perm, pressure, loglik = pl.pallas_call(
+        kernel,
+        out_shape=(
+            jax.ShapeDtypeStruct((FIELD, N), F32),
+            jax.ShapeDtypeStruct((FIELD, N), F32),
+            jax.ShapeDtypeStruct((1, 1), F32),
+        ),
+        in_specs=[smem] * 3 + [vmem] * 13,
+        out_specs=(vmem, vmem, smem),
         scratch_shapes=[
             pltpu.VMEM((512, 512), BF16),
             pltpu.VMEM((512, 512), BF16),
@@ -375,72 +624,32 @@
             pltpu.VMEM((8, KS, 128), F32),
             pltpu.VMEM((512, 128), F32),
             pltpu.VMEM((512, 128), F32),
-            pltpu.SemaphoreType.DMA((4,)),
+            pltpu.VMEM((256, 512), F32),
+            pltpu.VMEM((256, 128), F32),
+            pltpu.VMEM((8, 256, 1024), BF16),
+            pltpu.VMEM((512, 1024), BF16),
+            pltpu.VMEM((384, 256), BF16),
+            pltpu.VMEM((8, 128), F32),
+            field,
+            field,
+            field,
+            pltpu.VMEM((4, 32, N), F32),
+            pltpu.VMEM((FIELD, N), F32),
+            field,
+            field,
+            field,
+            field,
+            pltpu.VMEM((2, 8, 128), F32),
+            pltpu.VMEM((2, DEVICES, 128), F32),
+            pltpu.SemaphoreType.DMA((16,)),
         ],
         compiler_params=pltpu.CompilerParams(collective_id=0, has_side_effects=True, vmem_limit_bytes=60 * 2**20),
-    )(step, sigma, wave, state, noise, *[jnp.asarray(t) for t in tables()])
-
-
-def padded(block):
-    forward = [(i, i + 1) for i in range(DEVICES - 1)]
-    backward = [(i + 1, i) for i in range(DEVICES - 1)]
-    low = lax.ppermute(block[-1:], AXIS, forward)
-    high = lax.ppermute(block[:1], AXIS, backward)
-    return jnp.concatenate([low, block, high], axis=0)
-
-
-def body(state, noise, step, field_scale, wave_scale, source, obs_cells, obs_values):
-    position = lax.axis_index(AXIS)
-    log_perm = log_permeability(step, field_scale, wave_scale, state, noise)
-    kappa = jnp.exp(log_perm)
-    rimmed = padded(kappa)
-    sided = jnp.pad(kappa, ((0, 0), (1, 1)))
-    north = 0.5 * (kappa + rimmed[:-2])
-    south = 0.5 * (kappa + rimmed[2:])
-    west = 0.5 * (kappa + sided[:, :-2])
-    east = 0.5 * (kappa + sided[:, 2:])
-    diagonal = north + south + west + east
-    pressure = jnp.zeros_like(source)
-    residual = source
-    direction = jnp.zeros_like(source)
-    along = jnp.zeros_like(source)
-    gamma_prior = jnp.float32(1.0)
-    alpha_prior = jnp.float32(1.0)
-    for iteration in range(4):
-        precond = residual / diagonal
-        beside_all = padded(precond)
-        beside = jnp.pad(precond, ((0, 0), (1, 1)))
-        image = (
-            diagonal * precond
-            - north * beside_all[:-2]
-            - south * beside_all[2:]
-            - west * beside[:, :-2]
-            - east * beside[:, 2:]
-        )
-        gamma, delta = lax.psum(jnp.stack([jnp.sum(residual * precond), jnp.sum(precond * image)]), AXIS)
-        if iteration == 0:
-            alpha = gamma / delta
-            direction = precond
-            along = image
-        else:
-            ratio = gamma / gamma_prior
-            alpha = gamma / (delta - ratio * gamma / alpha_prior)
-            direction = precond + ratio * direction
-            along = image + ratio * along
-        pressure = pressure + alpha * direction
-        residual = residual - alpha * along
-        gamma_prior = gamma
-        alpha_prior = alpha
-    columns_here = pressure.shape[1]
-    cell_row = obs_cells // columns_here
-    cell_col = obs_cells % columns_here
-    local_row = cell_row - position * FIELD
-    inside = (local_row >= 0) & (local_row < FIELD)
-    picked = pressure[jnp.clip(local_row, 0, FIELD - 1), cell_col]
-    differ = jnp.where(inside, picked - obs_values, 0.0)
-    total = lax.psum(jnp.sum(differ * differ), AXIS)
-    loglik = -(2.0 / obs_cells.shape[0]) * total
-    return (log_perm, pressure, loglik)
+    )(
+        step, field_scale, wave_scale, state, noise, source,
+        obs_cells.reshape(64, 128), obs_values.reshape(64, 128),
+        *[jnp.asarray(t) for t in tables()],
+    )
+    return log_perm, pressure, loglik.reshape(())
 
 
 def solution(mesh):

time: 515 us -> 59.8 us (0.12)
  blocking collectives: 344 us -> 0 us
  local copies, waits for them, and re-layouts: 69 us -> 2.26 us
  starting transfers between devices: 24.9 us -> 0 us
  Pallas kernels: 33.8 us -> 53.1 us
  waiting for transfers between devices: 14.7 us -> 0 us
  between operations: 18.1 us -> 4.26 us
  other arithmetic: 9.36 us -> 0 us
    psum x5 -> x0, blocking collectives: 344 us -> none  [the longest x4 279 us: body(): lax.psum(jnp.stack([jnp.sum(residual * precond), jnp.sum(precond * image)...]
    gather x1 -> x0, local copies, waits for them, and re-layouts: 65 us -> none  [body(): picked = pressure[jnp.clip(local_row, 0, FIELD - 1), cell_col]]
    ppermute x10 -> x0, starting transfers between devices: 24.9 us -> none  [the longest x5 14.9 us: padded(): low = lax.ppermute(block[-1:], AXIS, forward)]
    pallas_call x1, Pallas kernels: 33.8 us -> 53.1 us  [body(): pl.pallas_call(kernel, out_shape=(jax.ShapeDtypeStruct((FIELD, N), F32),...]
    ppermute x10 -> x0, waiting for transfers between devices: 14.7 us -> none  [the longest x5 14.7 us: padded(): high = lax.ppermute(block[:1], AXIS, backward)]
    another operation x4 -> x0, other arithmetic: 5.37 us -> none  [body(): jnp.stack([jnp.sum(residual * precond), jnp.sum(precond * image)])]
  transfers between devices with their start and end apart: 10 -> 0, of which waited for: 5 -> 0; matrix products, arithmetic and copies ran while one was open for 0% -> 0% of each run, Pallas kernels for 0% -> 0%
where the time goes in v2:
time: 59.8 us; the launch traced here: 59.6 us
  Pallas kernels  53.1 us (89%)
  between operations  4.26 us (7%)
  local copies, waits for them, and re-layouts  2.26 us (4%)
    pallas_call x1, Pallas kernels, body(): pl.pallas_call(kernel, out_shape=(jax.ShapeDtypeStruct((FIELD, N), F32),...  53.1 us
    unnamed x4, local copies, waits for them, and re-layouts  2.26 us

profile of v2, /device:TPU:1, one launch (start us, length us, event | category | flops | bytes accessed | tf_op | source)
XLA Modules:
  0.0 59.6 jit_solution(4868565122323891713)
XLA Ops:
  2.6 53.1 %shard_map.175 = (f32[16,2048]{1,0:T(8,128)}, f32[16,2048]{1,0:T(8,128)}, f32[1,1]{1,0:T(1,128)}) custom-call(f32[1]{0:T(128)S(6)} %copy.22.step, f32[1]{0:T(128)S(6)} %copy.23.sigma, f32[1]{0:T(128)S(6)} %copy.24.wave, f32[32,4096]{1,0:T(8,128)} %state.1, f32[32,4096]{1,0:T(8,128)} %noise.1, f32[16,2048]{1,0:T(8,128)} %source.1, s32[64,128]{1,0:T(8,128)} %bitcast.3, ...), custom_call_target="tpu_custom_call" | custom-call | tf_op jit(solution)/shard_map/pallas_call | solution.py:610
  55.6 0.0 copy-start
  55.6 1.6 %copy.25 = f32[16,2048]{1,0:T(8,128)} copy(f32[16,2048]{1,0:T(8,128)} %get-tuple-element.12) | data formatting | bytes 262144
  57.2 0.0 copy-done
  57.3 0.7 %copy.26 = f32[16,2048]{1,0:T(8,128)} copy(f32[16,2048]{1,0:T(8,128)S(1)} %copy-done) | data formatting | bytes 262144
Async XLA Ops:
  55.6 1.6 %copy-start = (f32[16,2048]{1,0:T(8,128)S(1)}, f32[16,2048]{1,0:T(8,128)}, u32[]{:S(2)}) copy-start(f32[16,2048]{1,0:T(8,128)} %get-tuple-element.13) | copy-start | bytes 393220

commit v3 on v2

--- a/solution.py
+++ b/solution.py
@@ -61,7 +61,7 @@
     col_back = np.concatenate([np.cos(angle) * weight, -np.sin(angle) * weight], 1)
     r = np.arange(32)
     lanes_in = [(v, q) for v in range(4) for q in range(32)]
-    lanes_out = [(v, h * 16 + q) for h in range(2) for v in range(4) for q in range(16)]
+    lanes_out = [(v, h * 8 + q) for h in range(4) for v in range(4) for q in range(8)]
     turn = 2 * np.pi * np.outer(ks, [q for _, q in lanes_in]) / M
     turn_back = 2 * np.pi * np.outer(ks, [q for _, q in lanes_out]) / M
     col_turn = np.stack([np.cos(turn), np.sin(turn), np.cos(turn_back), np.sin(turn_back)])
@@ -283,8 +283,9 @@
         amp[v] = value
 
 
-def columns(got, amp, col_forward, col_back, col_turn, mid_forward, mid_back, out):
-    for u in range(4):
+def columns(half, got, amp, col_forward, col_back, col_turn, mid_forward, mid_back, out):
+    lane = lax.broadcasted_iota(jnp.int32, (64, 128), 1)
+    for u in (2 * half, 2 * half + 1):
         pieces = jnp.concatenate([got[pl.ds(2 * u + i, 128, stride=8), :] for i in range(2)], axis=1)
         spec = product((col_forward[0], col_forward[1]), split(pieces), NN)
         parts = []
@@ -304,34 +305,35 @@
             cos, sin = col_turn[2], col_turn[3]
             sides.append(jnp.concatenate([re * cos - im * sin, im * cos + re * sin], axis=0))
         field = product((col_back[0], col_back[1]), split(jnp.concatenate(sides, axis=1)), NN)
-        left, right = field[:, :128], field[:, 128:]
-        low = lax.broadcasted_iota(jnp.int32, (64, 128), 1) < 64
-        out[pl.ds(u, 64, stride=8), :] = jnp.where(low, left, pltpu.roll(right, 64, 1))
-        out[pl.ds(4 + u, 64, stride=8), :] = jnp.where(low, pltpu.roll(left, 64, 1), right)
+        for i in range(2):
+            here = field[:, 128 * i : 128 * i + 128]
+            later, sooner = pltpu.roll(here, 32, 1), pltpu.roll(here, 96, 1)
+            t = 2 * u + i
+            out[pl.ds(t, 64, stride=16), :] = jnp.where(lane < 32, pltpu.roll(later, 1, 0), later)
+            out[pl.ds(8 + t, 64, stride=16), :] = jnp.where(lane >= 96, pltpu.roll(sooner, 63, 0), sooner)
 
 
 def rows_back(got, row_back, row_turn, put):
-    blocks = [got[pl.ds(u, 128, stride=4), :].T for u in range(4)]
-    re = jnp.concatenate(blocks[:2], axis=0)
-    im = jnp.concatenate(blocks[2:], axis=0)
-    corner = (lax.broadcasted_iota(jnp.int32, (256, 128), 0) < FIELD) & (
-        lax.broadcasted_iota(jnp.int32, (256, 128), 1) == 0
-    )
-    top = jnp.broadcast_to(im[:FIELD, :1], (FIELD, 128))
-    sign = (1 - 2 * (lax.broadcasted_iota(jnp.int32, (FIELD, 128), 1) % 2)).astype(F32)
-    top = top * sign
-    im = jnp.where(corner, 0.0, im)
-    q = product(split(jnp.concatenate([re, im], axis=1)), (row_back[0], row_back[1]), NN)
+    blocks = [got[pl.ds(t, 128, stride=8), :].T for t in range(8)]
+    row = lax.broadcasted_iota(jnp.int32, (128, 128), 0)
+    lane = lax.broadcasted_iota(jnp.int32, (128, 128), 1)
+    sign = (1 - 2 * (lane[:8] % 2)).astype(F32)
+    tops = [jnp.broadcast_to(blocks[4][32 * g : 32 * g + 8, :1], (8, 128)) * sign for g in range(4)]
+    blocks[4] = jnp.where((row % 32 < 8) & (lane == 0), 0.0, blocks[4])
+    sides = jnp.concatenate([jnp.concatenate(blocks[:4], axis=0), jnp.concatenate(blocks[4:], axis=0)], axis=1)
+    q = product(split(sides), (row_back[0], row_back[1]), NN)
     for h in range(2):
-        zs = []
-        for kv in range(16):
-            rows = slice(FIELD * kv, FIELD * kv + FIELD)
-            zr, zi = q[rows, 128 * h : 128 * h + 128], q[rows, 256 + 128 * h : 384 + 128 * h]
-            cos = row_turn[0, kv : kv + 1, 128 * h : 128 * h + 128]
-            sin = row_turn[1, kv : kv + 1, 128 * h : 128 * h + 128]
-            zs.append((zr, zi) if kv == 0 else (zr * cos - zi * sin, zi * cos + zr * sin))
-        for a, value in enumerate(back_dft_real_first_half(zs)):
-            put(256 * a + 128 * h, value + top)
+        for g in range(4):
+            zs = []
+            for kv in range(16):
+                at = 128 * (kv // 4) + 32 * g + 8 * (kv % 4)
+                rows = slice(at, at + 8)
+                zr, zi = q[rows, 128 * h : 128 * h + 128], q[rows, 256 + 128 * h : 384 + 128 * h]
+                cos = row_turn[0, kv : kv + 1, 128 * h : 128 * h + 128]
+                sin = row_turn[1, kv : kv + 1, 128 * h : 128 * h + 128]
+                zs.append((zr, zi) if kv == 0 else (zr * cos - zi * sin, zi * cos + zr * sin))
+            for a, value in enumerate(back_dft_real_first_half(zs)):
+                put(8 * g, 256 * a + 128 * h, value + tops[g])
 
 
 def gather_observations(me, cells, values, counts, means, hot, parts):
@@ -494,9 +496,12 @@
 
 
 def lane_totals(sums):
-    rows = jnp.concatenate([jnp.sum(s, axis=0, keepdims=True) for s in sums], axis=0)
-    totals = jnp.broadcast_to(jnp.sum(rows, axis=1, keepdims=True), (8, 128))
-    at = lax.broadcasted_iota(jnp.int32, (8, 128), 0) == lax.broadcasted_iota(jnp.int32, (8, 128), 1)
+    count = len(sums)
+    high = -(-count // 8) * 8
+    rows = [jnp.sum(s, axis=0, keepdims=True) for s in sums] + [jnp.zeros((1, 128), F32)] * (high - count)
+    rows = jnp.concatenate(rows, axis=0)
+    totals = jnp.broadcast_to(jnp.sum(rows, axis=1, keepdims=True), (high, 128))
+    at = lax.broadcasted_iota(jnp.int32, (high, 128), 0) == lax.broadcasted_iota(jnp.int32, (high, 128), 1)
     return jnp.sum(jnp.where(at, totals, 0.0), axis=0, keepdims=True)
 
 
@@ -504,12 +509,51 @@
     mine[0:1, :] = row
     all_rows[pl.ds(me, 1), :] = row
     send_to_all(me, lambda d: mine.at[pl.ds(0, 1), :], lambda s: all_rows.at[pl.ds(s, 1), :], sems.at[0], sems.at[1])
+
+
+def shared(me, all_rows, sems):
     wait_for_all(me, all_rows.at[pl.ds(0, DEVICES - 1), :], sems.at[0], sems.at[1])
-    return jnp.sum(all_rows[...], axis=0, keepdims=True)
+
+
+PAIRS = [(i, j) for i in range(4) for j in range(i, 4)]
+
+
+def misfit_parts(guess, fields, counts, means, spread):
+    sums = [spread[...]] + [jnp.zeros((8, 128), F32) for _ in range(14)]
+    for j in range(TILES):
+        for g in range(2):
+            rows = slice(128 * g + 8 * j, 128 * g + 8 * j + 8)
+            us = [f[8 + 8 * g : 16 + 8 * g, tile(j)] for f in fields]
+            n = counts[rows, :128]
+            off = ((guess[0] * us[0] + guess[1] * us[1]) + (guess[2] * us[2] + guess[3] * us[3])) - means[rows, :]
+            many = n * off
+            sums[0] = sums[0] + many * off
+            for i in range(4):
+                sums[1 + i] = sums[1 + i] + many * us[i]
+            scaled_us = [n * u for u in us]
+            for k, (i, l) in enumerate(PAIRS):
+                sums[5 + k] = sums[5 + k] + scaled_us[i] * us[l]
+    row = lane_totals(sums)
+    lane = lax.broadcasted_iota(jnp.int32, (1, 128), 1)
+    for i in range(4):
+        row = jnp.where(lane == 15 + i, guess[i][:1], row)
+    return row
+
+
+def misfit(y, rows):
+    table = rows.T
+    off = [y[i][:1] - table[15 + i : 16 + i] for i in range(4)]
+    total = table[0:1]
+    for i in range(4):
+        total = total + 2.0 * off[i] * table[1 + i : 2 + i]
+    for k, (i, l) in enumerate(PAIRS):
+        term = off[i] * off[l] * table[5 + k : 6 + k]
+        total = total + (term if i == l else 2.0 * term)
+    return jnp.sum(total)
 
 
 def weights(row):
-    take = [jnp.broadcast_to(row[:, i : i + 1], (16, 128)) for i in range(8)]
+    take = [jnp.broadcast_to(row[:, i : i + 1], (8, 128)) for i in range(8)]
     g0, e0, m0, m1, q11, q12, q22, q23 = take
     m2 = 2.0 * q11 - m0
     m3 = 2.0 * q12 - m1
@@ -549,64 +593,103 @@
     return out
 
 
-def kernel(
-    step, sigma, wave, state, noise, source, cells, values,
-    row_forward, row_back, row_turn, col_forward, col_back, col_turn, mid_forward, mid_back,
-    log_perm, pressure, loglik,
-    z_high, z_low, sent1, got1, amp, sent2, got2,
-    counts, means, hot, parts, pieces, spread,
-    lx, sx, kappa, coefs, diag, v0, z0, z1, z2, mine, everyone, sems,
-):
+LOADS = ("state", "noise", "source", "cells", "values",
+         "row_forward", "row_back", "row_turn", "col_forward", "col_back", "col_turn", "mid_forward", "mid_back")
+
+
+def kernel(*refs):
+    (step, sigma, wave), refs = refs[:3], refs[3:]
+    count = len(LOADS)
+    sources, refs = refs[:count], refs[count:]
+    (log_perm_out, pressure_out, loglik), refs = refs[:3], refs[3:]
+    held, refs = refs[:count], refs[count:]
+    (
+        z_high, z_low, sent1, got1, amp, sent2, got2,
+        counts, means, hot, parts, pieces, spread,
+        lx, sx, kappa, coefs, diag, v0, z0, z1, z2, mine, everyone, pressure, sems, load_sems,
+    ) = refs
     me = lax.axis_index(AXIS)
+    loads = {
+        name: pltpu.make_async_copy(sources[k], held[k], load_sems.at[k]) for k, name in enumerate(LOADS)
+    }
+    for name in LOADS:
+        loads[name].start()
+    (state, noise, source, cells, values,
+     row_forward, row_back, row_turn, col_forward, col_back, col_turn, mid_forward, mid_back) = held
     greet_all(me)
+    for name in ("state", "noise", "row_turn", "row_forward"):
+        loads[name].wait()
     rows_forward(step[0], state, noise, row_turn, z_high, z_low, row_forward, sent1)
+    loads["source"].wait()
     meet_all()
-    send_to_all(me, lambda d: sent1.at[pl.ds(8 * d, 8), :], lambda s: got1.at[pl.ds(8 * s, 8), :], sems.at[0], sems.at[1])
-    source_edges = exchange_edges(me, source.at[pl.ds(0, 8), :], source.at[pl.ds(8, 8), :], sx, sems.at[pl.ds(4, 4)])
+    for half in range(2):
+        send_to_all(
+            me, lambda d: sent1.at[pl.ds(8 * d + 4 * half, 4), :], lambda s: got1.at[pl.ds(8 * s + 4 * half, 4), :],
+            sems.at[2 * half], sems.at[2 * half + 1],
+        )
+    source_edges = exchange_edges(me, source.at[pl.ds(0, 8), :], source.at[pl.ds(8, 8), :], sx, sems.at[pl.ds(8, 4)])
     for copy in source_edges:
         copy.start()
     own = pl.ds(pl.multiple_of(8 * me, 8), 8)
     got1[own, :] = sent1[own, :]
     sx[OWN, :] = source[...]
     amplitudes(me, sigma[0], wave[0], amp)
+    loads["cells"].wait()
+    loads["values"].wait()
     gather_observations(me, cells, values, counts, means, hot, parts)
-    wait_for_all(me, got1.at[pl.ds(0, 8 * (DEVICES - 1)), :], sems.at[0], sems.at[1])
-    columns(got1, amp, col_forward, col_back, col_turn, mid_forward, mid_back, sent2)
-    send_to_all(me, lambda d: sent2.at[pl.ds(4 * d, 4), :], lambda s: got2.at[pl.ds(4 * s, 4), :], sems.at[2], sems.at[3])
-    own = pl.ds(pl.multiple_of(4 * me, 4), 4)
+    for name in ("col_forward", "col_back", "col_turn", "mid_forward", "mid_back", "row_back"):
+        loads[name].wait()
+    for half in range(2):
+        wait_for_all(me, got1.at[pl.ds(0, 4 * (DEVICES - 1)), :], sems.at[2 * half], sems.at[2 * half + 1])
+        columns(half, got1, amp, col_forward, col_back, col_turn, mid_forward, mid_back, sent2)
+        send_to_all(
+            me, lambda d: sent2.at[pl.ds(8 * d + 4 * half, 4), :], lambda s: got2.at[pl.ds(8 * s + 4 * half, 4), :],
+            sems.at[4 + 2 * half], sems.at[5 + 2 * half],
+        )
     got2[own, :] = sent2[own, :]
     spread_observations(me, cells, values, means, hot, pieces, spread)
-    wait_for_all(me, got2.at[pl.ds(0, 4 * (DEVICES - 1)), :], sems.at[2], sems.at[3])
-
-    def put(at, value):
-        log_perm[:, at : at + 128] = value
-        lx[OWN, at : at + 128] = value
+    for half in range(2):
+        wait_for_all(me, got2.at[pl.ds(0, 4 * (DEVICES - 1)), :], sems.at[4 + 2 * half], sems.at[5 + 2 * half])
+
+    def put(row, at, value):
+        lx[row : row + 8, at : at + 128] = value
 
     rows_back(got2, row_back, row_turn, put)
-    edges = exchange_edges(me, lx.at[pl.ds(8, 8), :], lx.at[pl.ds(16, 8), :], lx, sems.at[pl.ds(8, 4)])
-    for copy in edges:
-        copy.start()
-    for copy in source_edges + edges:
+    write = pltpu.make_async_copy(lx.at[pl.ds(8, FIELD), :], log_perm_out, load_sems.at[count])
+    write.start()
+    for copy in source_edges:
         copy.wait()
     sums = krylov(me, lx, sx, kappa, coefs, diag, v0, z0, z1, z2)
-    y = weights(share(me, lane_totals(sums), mine.at[0], everyone.at[0], sems.at[pl.ds(12, 2)]))
-    total = spread[...]
+    row = lane_totals(sums)
+    share(me, row, mine.at[0], everyone.at[0], sems.at[pl.ds(12, 2)])
+    fields = (v0, z0, z1, z2)
+    guess = weights(row)
+    fine = jnp.abs(guess[0]) < 64.0
+    for i in range(1, 4):
+        fine = fine & (jnp.abs(guess[i]) < 64.0)
+    guess = [jnp.where(fine, g, 0.0) for g in guess]
+    share(me, misfit_parts(guess, fields, counts, means, spread), mine.at[1], everyone.at[1], sems.at[pl.ds(14, 2)])
+    shared(me, everyone.at[0], sems.at[pl.ds(12, 2)])
+    y = weights(jnp.sum(everyone[0], axis=0, keepdims=True))
     for j in range(TILES):
-        p = (y[0] * v0[OWN, tile(j)] + y[1] * z0[OWN, tile(j)]) + (y[2] * z1[OWN, tile(j)] + y[3] * z2[OWN, tile(j)])
-        pressure[:, tile(j)] = p
         for g in range(2):
-            rows = slice(128 * g + 8 * j, 128 * g + 8 * j + 8)
-            off = p[8 * g : 8 * g + 8] - means[rows, :]
-            total = total + counts[rows, :128] * (off * off)
-    misfit = jnp.sum(total, axis=0, keepdims=True)
-    everything = share(me, misfit, mine.at[1], everyone.at[1], sems.at[pl.ds(14, 2)])
-    loglik[0, 0] = F32(-2.0 / 8192) * jnp.sum(everything)
+            us = [f[8 + 8 * g : 16 + 8 * g, tile(j)] for f in fields]
+            pressure[8 * g : 8 * g + 8, tile(j)] = (y[0] * us[0] + y[1] * us[1]) + (y[2] * us[2] + y[3] * us[3])
+    write_pressure = pltpu.make_async_copy(pressure, pressure_out, load_sems.at[count + 1])
+    write_pressure.start()
+    shared(me, everyone.at[1], sems.at[pl.ds(14, 2)])
+    loglik[0, 0] = F32(-2.0 / 8192) * misfit(y, everyone[1])
+    write.wait()
+    write_pressure.wait()
 
 
 def body(state, noise, step, field_scale, wave_scale, source, obs_cells, obs_values):
-    vmem = pl.BlockSpec(memory_space=pltpu.VMEM)
+    anywhere = pl.BlockSpec(memory_space=pl.ANY)
     smem = pl.BlockSpec(memory_space=pltpu.SMEM)
     field = pltpu.VMEM((32, N), F32)
+    own = pltpu.VMEM((FIELD, N), F32)
+    arrays = [state, noise, source, obs_cells.reshape(64, 128), obs_values.reshape(64, 128)]
+    arrays += [jnp.asarray(t) for t in tables()]
     log_perm, pressure, loglik = pl.pallas_call(
         kernel,
         out_shape=(
@@ -614,16 +697,18 @@
             jax.ShapeDtypeStruct((FIELD, N), F32),
             jax.ShapeDtypeStruct((1, 1), F32),
         ),
-        in_specs=[smem] * 3 + [vmem] * 13,
-        out_specs=(vmem, vmem, smem),
+        in_specs=[pl.BlockSpec(memory_space=pltpu.SMEM)] * 3 + [anywhere] * len(arrays),
+        out_specs=(anywhere, anywhere, smem),
         scratch_shapes=[
+            pltpu.VMEM(a.shape, a.dtype) for a in arrays
+        ] + [
             pltpu.VMEM((512, 512), BF16),
             pltpu.VMEM((512, 512), BF16),
             pltpu.VMEM((1024, 128), F32),
             pltpu.VMEM((1024, 128), F32),
             pltpu.VMEM((8, KS, 128), F32),
-            pltpu.VMEM((512, 128), F32),
-            pltpu.VMEM((512, 128), F32),
+            pltpu.VMEM((1024, 128), F32),
+            pltpu.VMEM((1024, 128), F32),
             pltpu.VMEM((256, 512), F32),
             pltpu.VMEM((256, 128), F32),
             pltpu.VMEM((8, 256, 1024), BF16),
@@ -634,21 +719,19 @@
             field,
             field,
             pltpu.VMEM((4, 32, N), F32),
-            pltpu.VMEM((FIELD, N), F32),
+            own,
             field,
             field,
             field,
             field,
             pltpu.VMEM((2, 8, 128), F32),
             pltpu.VMEM((2, DEVICES, 128), F32),
+            own,
             pltpu.SemaphoreType.DMA((16,)),
+            pltpu.SemaphoreType.DMA((len(arrays) + 2,)),
         ],
-        compiler_params=pltpu.CompilerParams(collective_id=0, has_side_effects=True, vmem_limit_bytes=60 * 2**20),
-    )(
-        step, field_scale, wave_scale, state, noise, source,
-        obs_cells.reshape(64, 128), obs_values.reshape(64, 128),
-        *[jnp.asarray(t) for t in tables()],
-    )
+        compiler_params=pltpu.CompilerParams(collective_id=0, has_side_effects=True, vmem_limit_bytes=40 * 2**20),
+    )(step, field_scale, wave_scale, *[pltpu.with_memory_space_constraint(a, pltpu.HBM) for a in arrays])
     return log_perm, pressure, loglik.reshape(())
 
 

time: 59.8 us -> 49.6 us (0.83)
  Pallas kernels: 53.1 us -> 43.9 us
  local copies, waits for them, and re-layouts: 2.26 us -> 1.31 us
    pallas_call x1, Pallas kernels: 53.1 us -> 43.9 us  [body(): pl.pallas_call(kernel, out_shape=(jax.ShapeDtypeStruct((FIELD, N), F32),...]
    unnamed x4 -> x2, local copies, waits for them, and re-layouts: 2.26 us -> 1.31 us
where the time goes in v3:
time: 49.6 us; the launch traced here: 49.5 us
  Pallas kernels  43.9 us (89%)
  between operations  4.26 us (9%)
  local copies, waits for them, and re-layouts  1.31 us (3%)
    pallas_call x1, Pallas kernels, body(): pl.pallas_call(kernel, out_shape=(jax.ShapeDtypeStruct((FIELD, N), F32),...  43.9 us
    unnamed x2, local copies, waits for them, and re-layouts  1.31 us

profile of v3, /device:TPU:1, one launch (start us, length us, event | category | flops | bytes accessed | tf_op | source)
XLA Modules:
  0.0 49.5 jit_solution(12374970997232939963)
XLA Ops:
  2.6 43.9 %shard_map.175 = (f32[16,2048]{1,0:T(8,128)S(1)}, f32[16,2048]{1,0:T(8,128)S(1)}, f32[1,1]{1,0:T(1,128)}) custom-call(f32[1]{0:T(128)S(6)} %copy.22.refs_0_, f32[1]{0:T(128)S(6)} %copy.23.refs_1_, f32[1]{0:T(128)S(6)} %copy.24.refs_2_, f32[32,4096]{1,0:T(8,128)} %refs_3_.1, f32[32,4096]{1,0:T(8,128)} %refs_4_.1, f32[16,2048]{1,0:T(8,128)} %refs_5_.1, ...), custom_call_target="tpu_custom_call" | custom-call | tf_op jit(solution)/shard_map/pallas_call | solution.py:693
  46.5 0.7 %copy.25 = f32[16,2048]{1,0:T(8,128)} copy(f32[16,2048]{1,0:T(8,128)S(1)} %get-tuple-element.12) | data formatting | bytes 262144
  47.1 0.7 %copy.26 = f32[16,2048]{1,0:T(8,128)} copy(f32[16,2048]{1,0:T(8,128)S(1)} %get-tuple-element.13) | data formatting | bytes 262144

commit v4 on v3

--- a/solution.py
+++ b/solution.py
@@ -16,6 +16,8 @@
 ROWS = M // DEVICES
 FIELD = N // DEVICES
 KS = 80
+PARTS = 2
+PIECE = 8 // PARTS
 AXIS = "strip"
 MESH = pl.DeviceIdType.MESH
 F32 = jnp.float32
@@ -97,9 +99,14 @@
 
 
 def product(left, right, form):
-    dot = functools.partial(lax.dot_general, dimension_numbers=form, preferred_element_type=F32)
     (lh, ll), (rh, rl) = left, right
-    return dot(lh, rh) + (dot(lh, rl) + dot(ll, rh))
+    axis_left, axis_right = form[0][0][0], form[0][1][0]
+    return lax.dot_general(
+        jnp.concatenate([lh, lh, ll], axis=axis_left),
+        jnp.concatenate([rh, rl, rh], axis=axis_right),
+        dimension_numbers=form,
+        preferred_element_type=F32,
+    )
 
 
 def scaled(x, factor):
@@ -183,9 +190,9 @@
 
 
 def send_to_all(me, piece, landing, send_sem, recv_sem):
-    @pl.loop(1, DEVICES)
-    def _(i):
-        other = lax.rem(me + i, DEVICES)
+    for i in range(1, DEVICES):
+        other = me + i
+        other = jnp.where(other >= DEVICES, other - DEVICES, other)
         pltpu.make_async_remote_copy(
             src_ref=piece(other),
             dst_ref=landing(me),
@@ -283,9 +290,9 @@
         amp[v] = value
 
 
-def columns(half, got, amp, col_forward, col_back, col_turn, mid_forward, mid_back, out):
+def columns(part, got, amp, col_forward, col_back, col_turn, mid_forward, mid_back, out):
     lane = lax.broadcasted_iota(jnp.int32, (64, 128), 1)
-    for u in (2 * half, 2 * half + 1):
+    for u in range(4 // PARTS * part, 4 // PARTS * (part + 1)):
         pieces = jnp.concatenate([got[pl.ds(2 * u + i, 128, stride=8), :] for i in range(2)], axis=1)
         spec = product((col_forward[0], col_forward[1]), split(pieces), NN)
         parts = []
@@ -365,34 +372,29 @@
     means[...] = total / jnp.maximum(number, 1.0)
 
 
-def spread_observations(me, cells, values, means, hot, pieces, spread):
+def spread_observations(me, cells, values, means, hot, spread):
     turned_means = jnp.concatenate([means[:128, :].T, means[128:, :].T], axis=1)
-    high = turned_means.astype(BF16)
-    rest = turned_means - high.astype(F32)
-    middle = rest.astype(BF16)
-    pieces[:128, :] = high
-    pieces[128:256, :] = middle
-    pieces[256:, :] = (rest - middle.astype(F32)).astype(BF16)
+    pieces = jnp.concatenate(split(turned_means), axis=0)
     spread[...] = jnp.zeros_like(spread)
 
     @pl.loop(0, 8)
     def _(c):
-        picked = jnp.dot(pieces[...], hot[c], preferred_element_type=F32)
-        total = jnp.zeros((8, 128), F32)
-        for i in range(8):
-            cell = cells[pl.ds(8 * c + i, 1), :]
-            value = values[pl.ds(8 * c + i, 1), :]
-            row = cell // N - FIELD * me
-            inside = (row >= 0) & (row < FIELD)
-            lane = jnp.where(inside, cell % 128, -1)
-            lanes = slice(128 * i, 128 * i + 128)
-            mean = picked[:128, lanes] + (picked[128:256, lanes] + picked[256:, lanes])
-            there = lax.broadcasted_iota(jnp.int32, (128, 128), 0) == lane
-            off = jnp.where(there, value - mean, 0.0)
-            off = off * off
-            for k in range(16):
-                total = total + off[8 * k : 8 * k + 8]
-        spread[...] += total
+        totals = [jnp.zeros((8, 128), F32) for _ in range(4)]
+        for b in range(4):
+            picked = jnp.dot(pieces, hot[c, :, 256 * b : 256 * b + 256], preferred_element_type=F32)
+            for i in range(2):
+                cell = cells[pl.ds(8 * c + 2 * b + i, 1), :]
+                value = values[pl.ds(8 * c + 2 * b + i, 1), :]
+                row = cell // N - FIELD * me
+                lane = jnp.where((row >= 0) & (row < FIELD), cell % 128, -1)
+                lanes = slice(128 * i, 128 * i + 128)
+                mean = picked[:128, lanes] + picked[128:, lanes]
+                there = lax.broadcasted_iota(jnp.int32, (128, 128), 0) == lane
+                off = jnp.where(there, value - mean, 0.0)
+                off = off * off
+                for k in range(16):
+                    totals[k % 4] = totals[k % 4] + off[8 * k : 8 * k + 8]
+        spread[...] += (totals[0] + totals[1]) + (totals[2] + totals[3])
 
 
 def exchange_edges(me, own_low, own_high, ext, sems):
@@ -537,11 +539,11 @@
     lane = lax.broadcasted_iota(jnp.int32, (1, 128), 1)
     for i in range(4):
         row = jnp.where(lane == 15 + i, guess[i][:1], row)
-    return row
+    return pltpu.roll(jnp.broadcast_to(row, (8, 128)), 8, 1)[:1]
 
 
 def misfit(y, rows):
-    table = rows.T
+    table = rows.T[8:]
     off = [y[i][:1] - table[15 + i : 16 + i] for i in range(4)]
     total = table[0:1]
     for i in range(4):
@@ -605,51 +607,56 @@
     held, refs = refs[:count], refs[count:]
     (
         z_high, z_low, sent1, got1, amp, sent2, got2,
-        counts, means, hot, parts, pieces, spread,
-        lx, sx, kappa, coefs, diag, v0, z0, z1, z2, mine, everyone, pressure, sems, load_sems,
+        counts, means, hot, parts, spread,
+        lx, sx, kappa, coefs, diag, v0, z0, z1, z2, mine, everyone, pressure, sems, load_sems, edge_sems, end_sems,
     ) = refs
     me = lax.axis_index(AXIS)
     loads = {
         name: pltpu.make_async_copy(sources[k], held[k], load_sems.at[k]) for k, name in enumerate(LOADS)
     }
-    for name in LOADS:
+    early = ("state", "noise", "row_turn", "row_forward")
+    for name in early:
         loads[name].start()
     (state, noise, source, cells, values,
      row_forward, row_back, row_turn, col_forward, col_back, col_turn, mid_forward, mid_back) = held
     greet_all(me)
-    for name in ("state", "noise", "row_turn", "row_forward"):
+    for name in early:
         loads[name].wait()
+    for name in LOADS:
+        if name not in early:
+            loads[name].start()
     rows_forward(step[0], state, noise, row_turn, z_high, z_low, row_forward, sent1)
     loads["source"].wait()
     meet_all()
-    for half in range(2):
+    for part in range(PARTS):
         send_to_all(
-            me, lambda d: sent1.at[pl.ds(8 * d + 4 * half, 4), :], lambda s: got1.at[pl.ds(8 * s + 4 * half, 4), :],
-            sems.at[2 * half], sems.at[2 * half + 1],
+            me, lambda d: sent1.at[pl.ds(8 * d + PIECE * part, PIECE), :],
+            lambda s: got1.at[pl.ds(8 * s + PIECE * part, PIECE), :], sems.at[2 * part], sems.at[2 * part + 1],
         )
-    source_edges = exchange_edges(me, source.at[pl.ds(0, 8), :], source.at[pl.ds(8, 8), :], sx, sems.at[pl.ds(8, 4)])
+    source_edges = exchange_edges(me, source.at[pl.ds(0, 8), :], source.at[pl.ds(8, 8), :], sx, edge_sems)
     for copy in source_edges:
         copy.start()
     own = pl.ds(pl.multiple_of(8 * me, 8), 8)
     got1[own, :] = sent1[own, :]
     sx[OWN, :] = source[...]
     amplitudes(me, sigma[0], wave[0], amp)
-    loads["cells"].wait()
-    loads["values"].wait()
+    for name in ("col_forward", "col_back", "col_turn", "mid_forward", "mid_back", "row_back", "cells", "values"):
+        loads[name].wait()
     gather_observations(me, cells, values, counts, means, hot, parts)
-    for name in ("col_forward", "col_back", "col_turn", "mid_forward", "mid_back", "row_back"):
-        loads[name].wait()
-    for half in range(2):
-        wait_for_all(me, got1.at[pl.ds(0, 4 * (DEVICES - 1)), :], sems.at[2 * half], sems.at[2 * half + 1])
-        columns(half, got1, amp, col_forward, col_back, col_turn, mid_forward, mid_back, sent2)
+    for part in range(PARTS):
+        wait_for_all(me, got1.at[pl.ds(0, PIECE * (DEVICES - 1)), :], sems.at[2 * part], sems.at[2 * part + 1])
+        columns(part, got1, amp, col_forward, col_back, col_turn, mid_forward, mid_back, sent2)
         send_to_all(
-            me, lambda d: sent2.at[pl.ds(8 * d + 4 * half, 4), :], lambda s: got2.at[pl.ds(8 * s + 4 * half, 4), :],
-            sems.at[4 + 2 * half], sems.at[5 + 2 * half],
+            me, lambda d: sent2.at[pl.ds(8 * d + PIECE * part, PIECE), :],
+            lambda s: got2.at[pl.ds(8 * s + PIECE * part, PIECE), :],
+            sems.at[2 * (PARTS + part)], sems.at[2 * (PARTS + part) + 1],
         )
     got2[own, :] = sent2[own, :]
-    spread_observations(me, cells, values, means, hot, pieces, spread)
-    for half in range(2):
-        wait_for_all(me, got2.at[pl.ds(0, 4 * (DEVICES - 1)), :], sems.at[4 + 2 * half], sems.at[5 + 2 * half])
+    spread_observations(me, cells, values, means, hot, spread)
+    for part in range(PARTS):
+        wait_for_all(
+            me, got2.at[pl.ds(0, PIECE * (DEVICES - 1)), :], sems.at[2 * (PARTS + part)], sems.at[2 * (PARTS + part) + 1]
+        )
 
     def put(row, at, value):
         lx[row : row + 8, at : at + 128] = value
@@ -661,26 +668,36 @@
         copy.wait()
     sums = krylov(me, lx, sx, kappa, coefs, diag, v0, z0, z1, z2)
     row = lane_totals(sums)
-    share(me, row, mine.at[0], everyone.at[0], sems.at[pl.ds(12, 2)])
     fields = (v0, z0, z1, z2)
     guess = weights(row)
     fine = jnp.abs(guess[0]) < 64.0
     for i in range(1, 4):
         fine = fine & (jnp.abs(guess[i]) < 64.0)
     guess = [jnp.where(fine, g, 0.0) for g in guess]
-    share(me, misfit_parts(guess, fields, counts, means, spread), mine.at[1], everyone.at[1], sems.at[pl.ds(14, 2)])
-    shared(me, everyone.at[0], sems.at[pl.ds(12, 2)])
-    y = weights(jnp.sum(everyone[0], axis=0, keepdims=True))
+    share(me, row + misfit_parts(guess, fields, counts, means, spread), mine, everyone, end_sems)
+    shared(me, everyone, end_sems)
+    y = weights(jnp.sum(everyone[...], axis=0, keepdims=True))
     for j in range(TILES):
         for g in range(2):
             us = [f[8 + 8 * g : 16 + 8 * g, tile(j)] for f in fields]
             pressure[8 * g : 8 * g + 8, tile(j)] = (y[0] * us[0] + y[1] * us[1]) + (y[2] * us[2] + y[3] * us[3])
     write_pressure = pltpu.make_async_copy(pressure, pressure_out, load_sems.at[count + 1])
     write_pressure.start()
-    shared(me, everyone.at[1], sems.at[pl.ds(14, 2)])
-    loglik[0, 0] = F32(-2.0 / 8192) * misfit(y, everyone[1])
+    loglik[0, 0] = F32(-2.0 / 8192) * misfit(y, everyone[...])
     write.wait()
     write_pressure.wait()
+
+
+def finish(log_perm, pressure, loglik, log_perm_out, pressure_out, loglik_out, sems):
+    copies = [
+        pltpu.make_async_copy(log_perm, log_perm_out, sems.at[0]),
+        pltpu.make_async_copy(pressure, pressure_out, sems.at[1]),
+    ]
+    for copy in copies:
+        copy.start()
+    loglik_out[0, 0] = loglik[0, 0]
+    for copy in copies:
+        copy.wait()
 
 
 def body(state, noise, step, field_scale, wave_scale, source, obs_cells, obs_values):
@@ -713,7 +730,6 @@
             pltpu.VMEM((256, 128), F32),
             pltpu.VMEM((8, 256, 1024), BF16),
             pltpu.VMEM((512, 1024), BF16),
-            pltpu.VMEM((384, 256), BF16),
             pltpu.VMEM((8, 128), F32),
             field,
             field,
@@ -724,14 +740,28 @@
             field,
             field,
             field,
-            pltpu.VMEM((2, 8, 128), F32),
-            pltpu.VMEM((2, DEVICES, 128), F32),
+            pltpu.VMEM((8, 128), F32),
+            pltpu.VMEM((DEVICES, 128), F32),
             own,
-            pltpu.SemaphoreType.DMA((16,)),
+            pltpu.SemaphoreType.DMA((4 * PARTS,)),
             pltpu.SemaphoreType.DMA((len(arrays) + 2,)),
+            pltpu.SemaphoreType.DMA((4,)),
+            pltpu.SemaphoreType.DMA((2,)),
         ],
         compiler_params=pltpu.CompilerParams(collective_id=0, has_side_effects=True, vmem_limit_bytes=40 * 2**20),
     )(step, field_scale, wave_scale, *[pltpu.with_memory_space_constraint(a, pltpu.HBM) for a in arrays])
+    log_perm, pressure, loglik = pl.pallas_call(
+        finish,
+        out_shape=(
+            jax.ShapeDtypeStruct((FIELD, N), F32),
+            jax.ShapeDtypeStruct((FIELD, N), F32),
+            jax.ShapeDtypeStruct((1, 1), F32),
+        ),
+        in_specs=[anywhere, anywhere, smem],
+        out_specs=(anywhere, anywhere, smem),
+        scratch_shapes=[pltpu.SemaphoreType.DMA((2,))],
+        compiler_params=pltpu.CompilerParams(vmem_limit_bytes=2**20),
+    )(log_perm, pressure, loglik)
     return log_perm, pressure, loglik.reshape(())
 
 

time: 49.6 us -> 45.5 us (0.917)
  between operations: 4.26 us -> 2.58 us
  local copies, waits for them, and re-layouts: 1.31 us -> 0 us
  Pallas kernels: 43.9 us -> 42.8 us
    pallas_call x1, Pallas kernels: 43.9 us -> 40.9 us  [body(): pl.pallas_call(kernel, out_shape=(jax.ShapeDtypeStruct((FIELD, N), F32),...]
    pallas_call x0 -> x1, Pallas kernels: none -> 1.86 us  [body(): pl.pallas_call(finish, out_shape=(jax.ShapeDtypeStruct((FIELD, N), F32),...]
    unnamed x2 -> x0, local copies, waits for them, and re-layouts: 1.31 us -> none
where the time goes in v4:
time: 45.5 us; the launch traced here: 45.4 us
  Pallas kernels  42.8 us (94%)
  between operations  2.58 us (6%)
    pallas_call x1, Pallas kernels, body(): pl.pallas_call(kernel, out_shape=(jax.ShapeDtypeStruct((FIELD, N), F32),...  40.9 us
    pallas_call x1, Pallas kernels, body(): pl.pallas_call(finish, out_shape=(jax.ShapeDtypeStruct((FIELD, N), F32),...  1.86 us

profile of v4, /device:TPU:1, one launch (start us, length us, event | category | flops | bytes accessed | tf_op | source)
XLA Modules:
  0.0 45.4 jit_solution(12396180786618780757)
XLA Ops:
  2.6 40.9 %shard_map.175 = (f32[16,2048]{1,0:T(8,128)S(1)}, f32[16,2048]{1,0:T(8,128)S(1)}, f32[1,1]{1,0:T(1,128)}) custom-call(f32[1]{0:T(128)S(6)} %copy.19.refs_0_, f32[1]{0:T(128)S(6)} %copy.20.refs_1_, f32[1]{0:T(128)S(6)} %copy.21.refs_2_, f32[32,4096]{1,0:T(8,128)} %refs_3_.1, f32[32,4096]{1,0:T(8,128)} %refs_4_.1, f32[16,2048]{1,0:T(8,128)} %refs_5_.1, ...), custom_call_target="tpu_custom_call" | custom-call | tf_op jit(solution)/shard_map/pallas_call | solution.py:710
  43.5 1.9 %shard_map.176 = (f32[16,2048]{1,0:T(8,128)}, f32[16,2048]{1,0:T(8,128)}, f32[1,1]{1,0:T(1,128)}) custom-call(f32[16,2048]{1,0:T(8,128)S(1)} %get-tuple-element.9.log_perm, f32[16,2048]{1,0:T(8,128)S(1)} %get-tuple-element.10.pressure, f32[1,1]{1,0:T(1,128)} %get-tuple-element.11.loglik), custom_call_target="tpu_custom_call" | custom-call | tf_op jit(solution)/shard_map/pallas_call | solution.py:753
